TPU v7x, 128 devices: a whole 4x4x4 slice. The times are simulated.
128 devices in a mesh: seq: 16 (over x, y), head: 8 (over z, core).
Axes of the slice: x: 4, y: 4, z: 4, core: 2. Of those that a mesh axis runs over, the one named last changes fastest.
Arguments:
- query_rows: bfloat16 [65536, 2048], P(('seq', 'head')), may hold values from -6 to 6
- key_rows: bfloat16 [65536, 2048], P(('seq', 'head')), may hold values from -6 to 6
- value_rows: bfloat16 [65536, 2048], P(('seq', 'head')), may hold values from -6 to 6
- gate_rows: bfloat16 [65536, 2048], P(('seq', 'head')), may hold values from -6 to 6
- segment_ids: int32 [512], P('seq'), may hold values from 0 to 3, as said below
- decay_rates: float32 [16], replicated, may hold values from 7.6293946e-07 to 0.00030517578
- norm_gain: float32 [2048], replicated, may hold values from 0.25 to 1.75
- out_weight: bfloat16 [2048, 2048], P(('seq', 'head')), may hold values from -0.125 to 0.125
Outputs:
- mixed_out: bfloat16 [65536, 2048], P(('seq', 'head'))
Inputs may be any that keep to these rules, and one draw needn't show every extreme that they name: segment_ids never falls from one block to the next; every document number appears, each document spans 1 to 256 blocks and one spans exactly 256.
All inputs are finite; a program needn't handle non-finite values.
Results may differ from a plain program's by a relative error of at most 0.006.
Values may be sent and summed in bfloat16 or wider, within the bound.
A program may use at most 256 MiB of HBM per device.

v0:
```python
import jax
import jax.numpy as jnp
from jax import lax
from jax.sharding import Mesh
from jax.sharding import PartitionSpec as P

BLK = 128
SBLK = 512
HEAD = ("head_0", "head_1")
SEQ_HEAD = ("seq_0", "seq_1", "head_0", "head_1")
SEQ = ("seq_0", "seq_1")


three_pass = lax.Precision.HIGH


def neutral_like(array, identity):
    return jax.tree.map(
        lambda a, e: jnp.broadcast_to(jnp.asarray(e, a.dtype), a.shape), array, identity
    )


def prefix_by_axis(array, axes, combine, identity):
    before = start = neutral_like(array, identity)
    subtotal = array
    for axis in reversed(axes):
        count, index = (lax.axis_size(axis), lax.axis_index(axis))
        pieces = jax.tree.map(lambda part: lax.all_gather(part, axis), subtotal)
        inside, subtotal = (start, start)
        for k in range(count):
            passed = k < index
            subtotal = combine(subtotal, jax.tree.map(lambda part: part[k], pieces))
            inside = jax.tree.map(lambda new, old: jnp.where(passed, new, old), subtotal, inside)
        before = combine(inside, before)
    return before


def attend_local(queries, keys_here, values_here, tok_seg, rates_local):
    tok_count, head_count, head_width = queries.shape
    blocks = tok_count // SBLK
    positions = jnp.arange(SBLK, dtype=jnp.float32)
    offsets = positions[:, None] - positions[None, :]
    causal = offsets >= 0
    lagged = jnp.exp(-rates_local[:, None, None] * jnp.maximum(offsets, 0.0)[None])
    reach_base = jnp.exp(-rates_local[None, :] * (positions[:, None] + 1.0))
    keep_base = jnp.exp(-rates_local[None, :] * (SBLK - 1.0 - positions[:, None]))
    block_decay = jnp.exp(-rates_local * SBLK)

    def advance(carried, blocks_in):
        state_now, prev_seg = carried
        query_part, key_part, value_part, seg_part = blocks_in
        same_doc = (seg_part[:, None] == seg_part[None, :]) & causal
        scores = jnp.einsum(
            "ihd,jhd->hij", query_part, key_part, preferred_element_type=jnp.float32
        )
        weights = jnp.where(same_doc[None], scores * lagged, 0.0).astype(jnp.bfloat16)
        inner_part = jnp.einsum(
            "hij,jhd->ihd", weights, value_part, preferred_element_type=jnp.float32
        )
        reach_row = jnp.where((seg_part == prev_seg)[:, None], reach_base, 0.0)
        outer_part = reach_row[:, :, None] * jnp.einsum(
            "ihd,hde->ihe", query_part.astype(jnp.float32), state_now, precision=three_pass
        )
        last_seg = seg_part[-1]
        keep_row = jnp.where((seg_part == last_seg)[:, None], keep_base, 0.0)
        kept_keys = key_part.astype(jnp.float32) * keep_row[:, :, None]
        carry_keep = jnp.where(last_seg == prev_seg, block_decay, 0.0)
        new_state = carry_keep[:, None, None] * state_now + jnp.einsum(
            "jhd,jhe->hde", kept_keys, value_part.astype(jnp.float32), precision=three_pass
        )
        return ((new_state, last_seg), inner_part + outer_part)

    start = (
        jnp.zeros((head_count, head_width, head_width), jnp.float32),
        jnp.array(-1.0, jnp.float32),
    )
    shaped = (
        queries.reshape(blocks, SBLK, head_count, head_width),
        keys_here.reshape(blocks, SBLK, head_count, head_width),
        values_here.reshape(blocks, SBLK, head_count, head_width),
        tok_seg.reshape(blocks, SBLK),
    )
    finished, outputs = lax.scan(advance, start, shaped)
    return (outputs.reshape(tok_count, head_count, head_width), finished[0])


def add_carried(local_out, queries, tok_seg, rates_local, state_in, seg_in):
    positions = jnp.arange(queries.shape[0], dtype=jnp.float32)
    reach_row = jnp.where(
        (tok_seg == seg_in)[:, None],
        jnp.exp(-rates_local[None, :] * (positions[:, None] + 1.0)),
        0.0,
    )
    carried = jnp.einsum(
        "ihd,hde->ihe", queries.astype(jnp.float32), state_in, precision=three_pass
    )
    return (local_out + reach_row[:, :, None] * carried).astype(jnp.bfloat16)


def link_pieces(earlier, later):
    state_early, decay_early, first_early, last_early = earlier
    state_late, decay_late, first_late, last_late = later
    joined = (last_early == first_late) | (last_early < 0) | (first_late < 0)
    factor = jnp.where(joined, decay_late, 0.0)
    state_both = state_late + factor[:, None, None] * state_early
    decay_both = jnp.where(joined, decay_early * decay_late, 0.0)
    first_both = jnp.where(first_early < 0, first_late, first_early)
    last_both = jnp.where(last_late < 0, last_early, last_late)
    return (state_both, decay_both, first_both, last_both)


def summary_of(state_end, tok_seg, rates_local):
    tok_count = tok_seg.shape[0]
    whole_doc = jnp.where(tok_seg[0] == tok_seg[-1], jnp.exp(-rates_local * tok_count), 0.0)
    head_count = rates_local.shape[0]
    identity = (
        jnp.zeros_like(state_end),
        jnp.ones((head_count,), jnp.float32),
        -jnp.ones((1,), jnp.float32),
        -jnp.ones((1,), jnp.float32),
    )
    return ((state_end, whole_doc, tok_seg[:1], tok_seg[-1:]), identity)


def on_device(
    query_rows, key_rows, value_rows, gate_rows, segment_ids, decay_rates, norm_gain, out_weight
):
    tok_dev = query_rows.shape[0]
    head_total = decay_rates.shape[0]
    head_width = query_rows.shape[1] // head_total
    shaped = (
        query_rows.reshape(tok_dev, head_total, head_width),
        key_rows.reshape(tok_dev, head_total, head_width),
        value_rows.reshape(tok_dev, head_total, head_width),
    )
    blocks_dev = tok_dev // BLK
    own_ids = lax.dynamic_slice_in_dim(segment_ids, lax.axis_index(HEAD) * blocks_dev, blocks_dev)
    tok_seg = jnp.repeat(own_ids, BLK).astype(jnp.float32)
    queries, keys_here, values_here = shaped
    local_out, state_end = attend_local(queries, keys_here, values_here, tok_seg, decay_rates)
    summary, identity = summary_of(state_end, tok_seg, decay_rates)
    state_in, decay_in, first_in, last_in = prefix_by_axis(summary, SEQ_HEAD, link_pieces, identity)
    attention = add_carried(local_out, queries, tok_seg, decay_rates, state_in, last_in[0])
    widened = attention.astype(jnp.float32)
    inv_rms = lax.rsqrt(jnp.mean(widened * widened, axis=-1, keepdims=True) + 1e-06)
    normed = (widened * inv_rms).reshape(tok_dev, head_total * head_width)
    normed = (normed * norm_gain * jax.nn.silu(gate_rows.astype(jnp.float32))).astype(jnp.bfloat16)
    mixed_out = jnp.dot(
        normed,
        lax.all_gather(out_weight, SEQ_HEAD, axis=0, tiled=True),
        preferred_element_type=jnp.float32,
    )
    return mixed_out.astype(jnp.bfloat16)


def solution(mesh):
    split = Mesh(mesh.devices.reshape(4, 4, 4, 2), ("seq_0", "seq_1", "head_0", "head_1"))
    return jax.shard_map(
        on_device,
        mesh=split,
        in_specs=(
            P(SEQ_HEAD, None),
            P(SEQ_HEAD, None),
            P(SEQ_HEAD, None),
            P(SEQ_HEAD, None),
            P(SEQ),
            P(),
            P(),
            P(SEQ_HEAD, None),
        ),
        out_specs=P(SEQ_HEAD, None),
        check_vma=False,
    )
```

profile of v0, /device:TPU:1, one launch (start us, length us, event | category | flops | bytes accessed | tf_op | source)
XLA Modules:
  0.0 351.8 jit_solution(2318212796308319544)
XLA Ops:
  13.9 3.5 %all-reduce.13 = (f32[2]{0:T(128)S(1)}, f32[32]{0:T(128)S(1)}, f32[2]{0:T(128)S(1)}) all-reduce(f32[2]{0:T(128)S(1)} %slice_dynamic-update-slice_fusion.1, f32[32]{0:T(128)S(1)} %get-tuple-element.98, f32[2]{0:T(128)S(1)} %get-tuple-element.70), channel_id=2, replica_groups=mesh['seq_0'=4,'seq_1'=4,'head_0'=4,'head_1'=2] {'head_1'}, use_global_device_ids=true, to_apply=%add | all-reduce | flops 36 | bytes 288
  20.7 1.3 dynamic-slice.2
  22.7 1.4 dynamic-update-slice.1
  24.0 1.4 dynamic-update-slice.6
  25.6 9.8 %all-reduce.10 = (f32[4]{0:T(128)S(1)}, f32[64]{0:T(128)S(1)}, f32[4]{0:T(128)S(1)}) all-reduce(f32[4]{0:T(128)S(1)} %dynamic-update-slice.1, f32[64]{0:T(128)S(1)} %get-tuple-element.96, f32[4]{0:T(128)S(1)} %dynamic-update-slice.6), channel_id=3, replica_groups=mesh['seq_0'=4,'seq_1'=4,'head_0'=4,'head_1'=2] {'head_0'}, use_global_device_ids=true, to_apply=%add.1 | all-reduce | flops 72 | bytes 576
  36.0 1.2 fusion.156
  37.3 1.3 dynamic-slice.3
  42.3 1.3 dynamic-update-slice.8
  43.6 1.4 dynamic-update-slice.2
  45.0 8.7 %all-reduce.11 = (f32[4]{0:T(128)S(1)}, f32[4]{0:T(128)S(1)}) all-reduce(f32[4]{0:T(128)S(1)} %dynamic-update-slice.2, f32[4]{0:T(128)S(1)} %dynamic-update-slice.8), channel_id=4, replica_groups=mesh['seq_0'=4,'seq_1'=4,'head_0'=4,'head_1'=2] {'seq_1'}, use_global_device_ids=true, to_apply=%add.2 | all-reduce | flops 8 | bytes 64
  54.3 1.3 fusion.157
  60.7 1.3 dynamic-update-slice.9
  62.0 1.3 dynamic-update-slice.3
  63.3 8.4 %all-reduce.12 = (f32[4]{0:T(128)S(1)}, f32[4]{0:T(128)S(1)}) all-reduce(f32[4]{0:T(128)S(1)} %dynamic-update-slice.3, f32[4]{0:T(128)S(1)} %dynamic-update-slice.9), channel_id=5, replica_groups=mesh['seq_0'=4,'seq_1'=4,'head_0'=4,'head_1'=2] {'seq_0'}, use_global_device_ids=true, to_apply=%add.3 | all-reduce | flops 8 | bytes 64
  80.2 3.9 %copy.27 = bf16[512,2048]{0,1:T(8,128)(2,1)} copy(bf16[512,2048]{1,0:T(8,128)(2,1)} %param.9) | data formatting | bytes 4194304 | tf_op jit(solution)/shard_map/while/body/jit(dynamic_index_in_dim)/squeeze | solution.py:83
  84.2 4.7 %fusion.31 = f32[16,128,128]{2,1,0:T(8,128)} fusion(bf16[512,16,128]{0,2,1:T(8,128)(2,1)} %bitcast.288, f32[512,16]{0,1:T(8,128)S(1)} %get-tuple-element.100, f32[16]{0:T(128)S(1)} %get-tuple-element.97, bf16[512,2048]{1,0:T(8,128)(2,1)} %param.10), kind=kOutput, calls=%fused_computation.35 | convolution fusion | flops 807665664 | bytes 5275712 | tf_op jit(solution)/shard_map/while/body/eval_jaxpr/jhd,jhe->hde/dot_general | solution.py:68
  88.9 14.2 %all-gather.27.cloned.1.call-done = f32[32,128,128]{2,1,0:T(8,128)} async-done(((f32[16,128,128]{2,1,0:T(8,128)}), f32[32,128,128]{2,1,0:T(8,128)}) %all-gather.27.cloned.1.call-update) | async-done | bytes 2097168 | tf_op jit(solution)/shard_map/all_gather | solution.py:28
  103.1 2.8 fusion.53
  119.8 35.7 %all-gather.19.cloned.1.call-done = f32[4,16,128,128]{3,2,1,0:T(8,128)} async-done(((f32[1,16,128,128]{3,2,1,0:T(8,128)}), f32[4,16,128,128]{3,2,1,0:T(8,128)}) %all-gather.19.cloned.1.call-update) | async-done | bytes 4194320 | tf_op jit(solution)/shard_map/all_gather | solution.py:28
  155.5 3.6 %multiply_add_fusion.1 = f32[1,16,128,128]{3,2,1,0:T(8,128)} fusion(f32[4,16,128,128]{3,2,1,0:T(8,128)} %all-gather.19.cloned.1.call-done, f32[16]{0:T(128)S(1)} %get-tuple-element.93, f32[16]{0:T(128)S(1)} %get-tuple-element.92, f32[16]{0:T(128)S(1)} %get-tuple-element.91, f32[16]{0:T(128)S(1)} %get-tuple-element.77), kind=kLoop, calls=%fused_computation.77 | loop fusion | flops 1835008 | bytes 5243136 | tf_op jit(solution)/shard_map/add | solution.py:105
  169.5 8.4 %all-gather.11 = f32[4,1,16]{2,1,0:T(1,128)S(1)} all-gather(f32[1,1,16]{2,1,0:T(1,128)S(1)} %get-tuple-element.76), channel_id=1, replica_groups=mesh['seq_0'=4,'seq_1'=4,'head_0'=4,'head_1'=2] {'seq_1'}, dimensions={0}, use_global_device_ids=true | all-gather | bytes 320 | tf_op jit(solution)/shard_map/all_gather | solution.py:28
  177.9 29.8 %all-gather.21.cloned.1.call-done = f32[4,16,128,128]{3,2,1,0:T(8,128)} async-done(((f32[1,16,128,128]{3,2,1,0:T(8,128)}), f32[4,16,128,128]{3,2,1,0:T(8,128)}) %all-gather.21.cloned.1.call-update) | async-done | bytes 4194320 | tf_op jit(solution)/shard_map/all_gather | solution.py:28
  207.7 3.6 %multiply_add_fusion = f32[1,16,128,128]{3,2,1,0:T(8,128)} fusion(f32[4,16,128,128]{3,2,1,0:T(8,128)} %all-gather.21.cloned.1.call-done, f32[16]{0:T(128)S(1)} %get-tuple-element.68, f32[16]{0:T(128)S(1)} %get-tuple-element.69, f32[16]{0:T(128)S(1)} %get-tuple-element.67, f32[16]{0:T(128)S(1)} %get-tuple-element.66), kind=kLoop, calls=%fused_computation.70 | loop fusion | flops 1835008 | bytes 5243136 | tf_op jit(solution)/shard_map/add | solution.py:105
  216.2 7.8 %all-gather.12 = f32[4,1,16]{2,1,0:T(1,128)S(1)} all-gather(f32[1,1,16]{2,1,0:T(1,128)S(1)} %bitcast.290), channel_id=1, replica_groups=mesh['seq_0'=4,'seq_1'=4,'head_0'=4,'head_1'=2] {'seq_0'}, dimensions={0}, use_global_device_ids=true | all-gather | bytes 320 | tf_op jit(solution)/shard_map/all_gather | solution.py:28
  224.5 3.3 fusion.18
  227.8 10.0 %fusion.13 = f32[16,512,128]{1,2,0:T(8,128)} fusion(bf16[512,16,128]{0,2,1:T(8,128)(2,1)} %bitcast.289, f32[512,512]{1,0:T(8,128)S(1)} %fusion.80, f32[16]{0:T(128)S(1)} %get-tuple-element.99, pred[512,512]{1,0:T(8,128)(4,1)S(1)} %fusion.82, bf16[512,2048]{1,0:T(8,128)(2,1)} %param.10, bf16[512,2048]{1,0:T(8,128)(2,1)S(1)} %copy-done), kind=kOutput, calls=%fused_computation.20 | convolution fusion | flops 2164260864 | bytes 11796544 | tf_op jit(solution)/shard_map/while/body/eval_jaxpr/hij,jhd->ihd/dot_general | solution.py:57
  237.9 22.2 %all-gather.23.cloned.1.call-done = f32[4,16,128,128]{3,2,1,0:T(8,128)} async-done(((f32[1,16,128,128]{3,2,1,0:T(8,128)}), f32[4,16,128,128]{3,2,1,0:T(8,128)}) %all-gather.23.cloned.1.call-update) | async-done | bytes 4194320 | tf_op jit(solution)/shard_map/all_gather | solution.py:28
  260.0 11.3 %fusion = (f32[512,16]{0,1:T(8,128)S(1)}, bf16[512,16,128]{0,2,1:T(8,128)(2,1)}) fusion(f32[4,16,128,128]{3,2,1,0:T(8,128)} %all-gather.23.cloned.1.call-done, f32[4,16,128,128]{3,2,1,0:T(8,128)} %all-gather.21.cloned.1.call-done, f32[4,16,128,128]{3,2,1,0:T(8,128)} %all-gather.19.cloned.1.call-done, f32[32,128,128]{2,1,0:T(8,128)} %all-gather.27.cloned.1.call-done, ...), kind=kOutput, calls=%fused_computation.5 | convolution fusion | flops 825221120 | bytes 27362382 | tf_op jit(solution)/shard_map/ihd,hde->ihe/dot_general | solution.py:94
  271.3 4.1 %convert_multiply_fusion.1 = f32[512,16,128]{0,2,1:T(8,128)} fusion(bf16[512,16,128]{0,2,1:T(8,128)(2,1)} %get-tuple-element.125, f32[512,16]{0,1:T(8,128)S(1)} %add_rsqrt_fusion), kind=kLoop, calls=%fused_computation.3 | loop fusion | flops 2097152 | bytes 6324224 | tf_op jit(solution)/shard_map/mul | solution.py:146
  275.4 5.4 %copy.24 = f32[512,2048]{1,0:T(8,128)} copy(f32[512,2048]{0,1:T(8,128)} %bitcast.287) | data formatting | bytes 8388608 | tf_op jit(solution)/shard_map/reshape | solution.py:146
  280.8 53.0 %all-gather.25.cloned.1.call-done = bf16[2048,2048]{1,0:T(8,128)(2,1)} async-done(((bf16[16,2048]{1,0:T(8,128)(2,1)}), bf16[2048,2048]{1,0:T(8,128)(2,1)}) %all-gather.25.cloned.1.call-update) | async-done | bytes 8388624 | tf_op jit(solution)/shard_map/all_gather | solution.py:150
  333.8 11.5 %convolution_convert_fusion = bf16[512,2048]{1,0:T(8,128)(2,1)} fusion(bf16[2048,2048]{1,0:T(8,128)(2,1)} %all-gather.25.cloned.1.call-done, bf16[512,2048]{1,0:T(8,128)(2,1)} %param.11, f32[512,2048]{1,0:T(8,128)} %copy.24, f32[2048]{0:T(1024)S(1)} %copy-done.1), kind=kOutput, calls=%fused_computation.19 | convolution fusion | flops 4304404480 | bytes 16785408 | tf_op jit(solution)/shard_map/dot_general | solution.py:148
  (53 shorter events, 15.5 us)
Async XLA Ops:
  6.5 218.0 %copy-start = (bf16[512,2048]{1,0:T(8,128)(2,1)S(1)}, bf16[512,2048]{1,0:T(8,128)(2,1)}, u32[]{:S(2)}) copy-start(bf16[512,2048]{1,0:T(8,128)(2,1)} %param.8) | copy-start | bytes 6291460
  6.5 96.6 %all-gather.27.cloned.1.call-start = ((), (), s32[]{:S(2)}) async-start(), calls=%async_computation.4 | async-start | bytes 3145728 | tf_op jit(solution)/shard_map/all_gather | solution.py:28
  88.8 66.6 %all-gather.19.cloned.1.call-start = ((), (), s32[]{:S(2)}) async-start(), calls=%async_computation | async-start | bytes 5242880 | tf_op jit(solution)/shard_map/all_gather | solution.py:28
  105.9 101.8 %all-gather.21.cloned.1.call-start = ((), (), s32[]{:S(2)}) async-start(), calls=%async_computation.1 | async-start | bytes 5242880 | tf_op jit(solution)/shard_map/all_gather | solution.py:28
  159.1 101.0 %all-gather.23.cloned.1.call-start = ((), (), s32[]{:S(2)}) async-start(), calls=%async_computation.2 | async-start | bytes 5242880 | tf_op jit(solution)/shard_map/all_gather | solution.py:28
  211.3 122.4 %all-gather.25.cloned.1.call-start = ((), (), s32[]{:S(2)}) async-start(), calls=%async_computation.3 | async-start | bytes 8454144 | tf_op jit(solution)/shard_map/all_gather | solution.py:150
  275.4 58.3 %copy-start.1 = (f32[2048]{0:T(1024)S(1)}, f32[2048]{0:T(1024)}, u32[]{:S(2)}) copy-start(f32[2048]{0:T(1024)} %param.14) | copy-start | bytes 24580
Sparse Core Ops, SparseCore 0:
  89.0 14.1 all-gather.26
  106.0 49.3 all-gather.18
  159.2 48.4 all-gather.20
  211.5 48.5 all-gather.22
  262.9 70.8 all-gather.24
where the time goes:
time: 353 us; the launch traced here: 352 us
  waiting for transfers between devices  155 us (44%)
  between operations  57.5 us (16%)
  blocking collectives  46.7 us (13%)
  matrix products  40.8 us (12%)
  local copies, waits for them, and re-layouts  25.8 us (7%)
  other arithmetic  25.5 us (7%)
    all_gather x4, waiting for transfers between devices, prefix_by_axis(): pieces = jax.tree.map(lambda part: lax.all_gather(part, axis), subtotal)  102 us
    all_gather x1, waiting for transfers between devices, on_device(): lax.all_gather(out_weight, SEQ_HEAD, axis=0, tiled=True)  53 us
    unnamed x4, blocking collectives  30.5 us
    all_gather x2, blocking collectives, prefix_by_axis(): pieces = jax.tree.map(lambda part: lax.all_gather(part, axis), subtotal)  16.2 us
    unnamed x26, local copies, waits for them, and re-layouts  15.2 us
    dot_general x1, matrix products, on_device(): jnp.dot(normed, lax.all_gather(out_weight, SEQ_HEAD, axis=0, tiled=True),...  11.5 us
    dot_general x1, matrix products, add_carried(): jnp.einsum('ihd,hde->ihe', queries.astype(jnp.float32), state_in, precisi...  11.3 us
    dot_general x1, matrix products, advance(): jnp.einsum('hij,jhd->ihd', weights, value_part, preferred_element_type=jn...  10 us
  transfers between devices with their start and end apart: 5, of which 5 were waited for; matrix products, arithmetic and copies ran while one was open for 10% of the time, Pallas kernels for 0%

commit v1 on v0

v1 whole, which is shorter than its diff:
```python
import functools

import jax
import jax.numpy as jnp
from jax import lax
from jax.experimental import pallas as pl
from jax.experimental.pallas import tpu as pltpu
from jax.sharding import Mesh
from jax.sharding import PartitionSpec as P

BLK = 128
SBLK = 512
DH = 128
FAR = 1e30
X, Y, Z, C = "seq_0", "seq_1", "head_0", "head_1"
SEQ_HEAD = (X, Y, Z, C)
SEQ = (X, Y)
MESH_ID = pl.DeviceIdType.MESH
F32, BF16 = jnp.float32, jnp.bfloat16

COLOURS = (
    (0, 768, (2, 1, 0)),
    (768, 640, (1, 0, 2)),
    (1408, 640, (0, 2, 1)),
)


def dot(a, b, ca, cb):
    return lax.dot_general(a, b, (((ca,), (cb,)), ((), ())), preferred_element_type=F32)


def same(a, b, n):
    return jnp.where(a == b, n, FAR)


def decay(rate, n):
    return jnp.exp(-rate * jnp.broadcast_to(n, (1, DH)))


def scan_kernel(
    ids, rates, q_hbm, k_hbm, v_hbm, g_hbm, gain, w_in,
    nrm_hbm, w_all,
    q, k, v, g, wbuf, nrm, inner, gated, offs0, offs1, keep_n, reach_n,
    s_own, s_out, s_in, z_out, z_in, p_part, y_out, y_in, x_out, x_in, p_out, p_in, c_out, c_in, p_own,
    load_sem, store_sem, c_send, c_recv, z_send, z_recv, y_send, y_recv, x_send, x_recv,
    p_send, p_recv, d_send, d_recv, w_send, w_recv, b_send, b_recv,
):
    at = (lax.axis_index(X), lax.axis_index(Y), lax.axis_index(Z))
    x, y, z = at
    c = lax.axis_index(C)
    names = (X, Y, Z)

    def near(axis, step):
        return lax.rem(at[axis] + step, 4)

    barrier = pltpu.get_barrier_semaphore()
    pl.semaphore_signal(barrier, inc=1, device_id={C: 1 - c}, device_id_type=MESH_ID)
    for axis in range(3):
        for step in (1, 2, 3):
            pl.semaphore_signal(
                barrier, inc=1, device_id={names[axis]: near(axis, step)}, device_id_type=MESH_ID
            )
    loads = [
        pltpu.make_async_copy(src, dst, load_sem.at[n])
        for n, (src, dst) in enumerate(
            ((k_hbm, k), (v_hbm, v), (w_in, wbuf), (q_hbm, q), (g_hbm, g))
        )
    ]
    for load in loads:
        load.start()

    place = z * 2 + c
    own_id = [ids[place * 4 + b] for b in range(4)]
    row = lax.broadcasted_iota(jnp.int32, (BLK, BLK), 0)
    column = lax.broadcasted_iota(jnp.int32, (BLK, BLK), 1)
    rows = row.astype(F32)
    ahead = (row - column).astype(F32)
    for bi in range(4):
        part = slice(bi * BLK, bi * BLK + BLK)
        keep_n[part, :] = (SBLK - 1.0 - bi * BLK) - rows + same(own_id[bi], own_id[3], 0.0)
        reach_n[part, :] = (1.0 + bi * BLK) + rows + same(own_id[bi], own_id[0], 0.0)
        for bj in range(4):
            if bj >= 2 and bi < 2:
                continue
            if bj > bi:
                block = jnp.full((BLK, BLK), FAR, F32)
            else:
                block = ahead + float(BLK * (bi - bj))
                if bi == bj:
                    block = jnp.where(ahead >= 0, block, FAR)
                block = block + same(own_id[bi], own_id[bj], 0.0)
            if bj < 2:
                offs0[part, bj * BLK : bj * BLK + BLK] = block
            else:
                offs1[bi * BLK - 256 : bi * BLK - 128, bj * BLK - 256 : bj * BLK - 128] = block

    def cols(h):
        return pl.ds(pl.multiple_of(h * DH, DH), DH)

    def states(into, first):
        @pl.loop(0, 8)
        def _(i):
            h = first + i
            kept = k[:, cols(h)].astype(F32) * jnp.exp(-rates[h] * keep_n[...])
            into[i] = dot(kept.astype(BF16), v[:, cols(h)], 0, 0)

    def attend(low, high):
        @pl.loop(low, high)
        def _(h):
            rate = rates[h]
            queries, keys, values = q[:, cols(h)], k[:, cols(h)], v[:, cols(h)]
            scores = dot(queries, keys[:256], 1, 1)
            weights = (scores * jnp.exp(-rate * offs0[...])).astype(BF16)
            total = dot(weights, values[:256], 1, 0)
            scores = dot(queries[256:], keys[256:], 1, 1)
            weights = (scores * jnp.exp(-rate * offs1[...])).astype(BF16)
            inner[h, :256, :] = total[:256]
            inner[h, 256:, :] = total[256:] + dot(weights, values[256:], 1, 0)
            gate = g[:, cols(h)].astype(F32)
            gated[h] = gain[:, cols(h)] * (gate / (1.0 + jnp.exp(-gate)))

    def remote(src, dst, send, recv, to):
        return pltpu.make_async_remote_copy(
            src_ref=src, dst_ref=dst, send_sem=send, recv_sem=recv, device_id=to, device_id_type=MESH_ID
        )

    def piece(colour, phase, coord, half):
        low, wide, order = COLOURS[colour]
        index = list(at) + [c]
        for axis in order[:phase]:
            index[axis] = slice(0, 4)
        index[order[phase]] = coord
        lanes = slice(low, low + wide)
        if half is not None:
            if phase == 0:
                cut = 384
                lanes = slice(low, low + cut) if half == 0 else slice(low + cut, low + wide)
            else:
                index[order[0]] = slice(2 * half, 2 * half + 2)
        return tuple(index) + (slice(None), lanes)

    started = []

    def ring_copy(colour, phase, slot, step, coord, half):
        axis = COLOURS[colour][2][phase]
        where = piece(colour, phase, coord, half)
        src = w_all.at[where]
        if phase == 0 and slot < 4:
            src = wbuf.at[where[-2:]]
        return remote(
            src, w_all.at[where], w_send.at[colour, phase, slot], w_recv.at[colour, phase, slot],
            {names[axis]: near(axis, step)},
        )

    SLOTS = ((1, 0), (1, 1), (3, 1), (3, 0), (1, 0), (3, 1))

    def ring_start(phase):
        for colour in range(3):
            mine = at[COLOURS[colour][2][phase]]
            for slot in (0, 2, 1, 3):
                step, half = SLOTS[slot]
                copy = ring_copy(colour, phase, slot, step, mine, half)
                copy.start()
                started.append(copy)

    def ring_pass(phase):
        for colour in range(3):
            axis = COLOURS[colour][2][phase]
            for slot in (0, 2):
                step, half = SLOTS[slot]
                from_coord = near(axis, 4 - step)
                ring_copy(colour, phase, slot, step, from_coord, half).wait_recv()
                copy = ring_copy(colour, phase, slot + 4 if slot == 0 else 5, step, from_coord, half)
                copy.start()
                started.append(copy)

    def twin_copy(where, slot):
        return remote(w_all.at[where], w_all.at[where], b_send.at[slot], b_recv.at[slot], {C: 1 - c})

    def other(where):
        return where[:3] + (1 - c,) + where[4:]

    twins = []

    def twin(where, slot):
        copy = twin_copy(where, slot)
        copy.start()
        started.append(copy)
        twins.append((other(where), slot))

    def ring_end(phase):
        for colour in range(3):
            axis = COLOURS[colour][2][phase]
            for slot in (1, 3):
                step, half = SLOTS[slot]
                ring_copy(colour, phase, slot, step, near(axis, 4 - step), half).wait_recv()
            base = (colour * 3 + phase) * 3
            twin(piece(colour, phase, near(axis, 1), None), base)
            twin(piece(colour, phase, near(axis, 3), None), base + 1)
        for colour in range(3):
            axis = COLOURS[colour][2][phase]
            for slot in (4, 5):
                step, half = SLOTS[slot]
                ring_copy(colour, phase, slot, step, near(axis, 2), half).wait_recv()
            twin(piece(colour, phase, near(axis, 2), None), (colour * 3 + phase) * 3 + 2)

    loads[0].wait()
    loads[1].wait()
    states(s_out, (1 - c) * 8)
    pl.semaphore_wait(barrier, 10)
    core_copy = remote(s_out, s_in, c_send, c_recv, {C: 1 - c})
    core_copy.start()
    loads[2].wait()
    ring_start(0)
    own_store = pltpu.make_async_copy(wbuf, w_all.at[x, y, z, c], store_sem.at[2])
    own_store.start()
    states(s_own, c * 8)
    core_copy.wait()

    chip = z * 8
    n_first = jnp.where(c == 0, same(ids[chip + 3], ids[chip + 7], 512.0), 0.0)
    n_second = jnp.where(c == 1, same(ids[chip + 3], ids[chip + 7], 512.0), 0.0)
    for i in range(8):
        rate = rates[c * 8 + i]
        both = s_own[i] * decay(rate, n_first) + s_in[i] * decay(rate, n_second)
        z_out[i // 2, (i % 2) * DH : (i % 2) * DH + DH, :] = both.astype(BF16)
    line_copies = []
    for step in (1, 3, 2):
        to = near(2, step)
        copy = remote(z_out.at[to], z_in.at[3 - step], z_send.at[step - 1], z_recv.at[3 - step], {Z: to})
        copy.start()
        line_copies.append(copy)
    loads[3].wait()
    loads[4].wait()
    ring_pass(0)
    attend(0, 2)
    for copy in line_copies:
        copy.wait()

    two = [rates[c * 8 + z * 2 + j] for j in range(2)]
    spots = [near(2, step) for step in range(4)]
    line_last = ids[31]

    def held(step, j):
        part = slice(j * DH, j * DH + DH)
        block = z_out[z, part, :] if step == 0 else z_in[step - 1, part, :]
        return block.astype(F32)

    for j in range(2):
        total = None
        for step in range(4):
            spot = spots[step]
            n = same(ids[spot * 8 + 7], line_last, (1024 * (3 - spot)).astype(F32))
            term = held(step, j) * decay(two[j], n)
            total = term if total is None else total + term
        y_out[j * DH : j * DH + DH, :] = total
    y_out[2 * DH : 2 * DH + 8, :] = jnp.broadcast_to(line_last.astype(F32), (8, DH))
    column_copies = []
    for step in (1, 3, 2):
        copy = remote(
            y_out, y_in.at[3 - step], y_send.at[step - 1], y_recv.at[3 - step], {Y: near(1, step)}
        )
        copy.start()
        column_copies.append(copy)
    own_store.wait()
    twin((x, y, z, c, slice(None), slice(None)), 27)
    ring_end(0)
    ring_start(1)
    for t in range(4):
        target = spots[t]
        for j in range(2):
            total = None
            for step in range(4):
                if step == t:
                    continue
                spot = spots[step]
                n = same(ids[spot * 8 + 7], ids[target * 8], (1024 * (target - 1 - spot)).astype(F32))
                term = held(step, j) * decay(two[j], jnp.where(spot < target, n, FAR))
                total = term if total is None else total + term
            p_part[t, j * DH : j * DH + DH, :] = total
    attend(2, 4)
    for copy in column_copies:
        copy.wait()

    def gathered(own, came, step):
        return own if step == 0 else came.at[step - 1]

    def note(ref):
        return ref[2 * DH : 2 * DH + 1, :]

    line_first = ids[0].astype(F32)
    spots_y = [near(1, step) for step in range(4)]
    last_note = jnp.zeros((1, DH), F32)
    for step in range(4):
        last_note = last_note + jnp.where(spots_y[step] == 3, 1.0, 0.0) * note(gathered(y_out, y_in, step))
    for j in range(2):
        part = slice(j * DH, j * DH + DH)
        total = None
        for step in range(4):
            ref, spot = gathered(y_out, y_in, step), spots_y[step]
            n = same(note(ref), last_note, (4096 * (3 - spot)).astype(F32))
            term = ref[part, :] * decay(two[j], n)
            total = term if total is None else total + term
        x_out[part, :] = total
    x_out[2 * DH : 2 * DH + 8, :] = jnp.broadcast_to(last_note, (8, DH))
    slab_copies = []
    for step in (1, 3, 2):
        copy = remote(
            x_out, x_in.at[3 - step], x_send.at[step - 1], x_recv.at[3 - step], {X: near(0, step)}
        )
        copy.start()
        slab_copies.append(copy)
    ring_pass(1)
    attend(4, 7)
    ring_end(1)
    ring_start(2)
    for copy in slab_copies:
        copy.wait()

    spots_x = [near(0, step) for step in range(4)]
    for j in range(2):
        part = slice(j * DH, j * DH + DH)
        total = jnp.zeros((DH, DH), F32)
        for step in range(1, 4):
            ref, spot = y_in.at[step - 1], spots_y[step]
            n = same(note(ref), line_first, (4096 * (y - 1 - spot)).astype(F32))
            total = total + ref[part, :] * decay(two[j], jnp.where(spot < y, n, FAR))
            ref, spot = x_in.at[step - 1], spots_x[step]
            n = same(note(ref), line_first, (16384 * (x - 1 - spot) + 4096 * y).astype(F32))
            total = total + ref[part, :] * decay(two[j], jnp.where(spot < x, n, FAR))
        for t in range(4):
            target = spots[t]
            n = same(ids[0], ids[target * 8], (1024 * target).astype(F32))
            p_out[t, part, :] = (p_part[t, part, :] + total * decay(two[j], n)).astype(BF16)
    back_copies = []
    for step in (1, 3, 2):
        copy = remote(
            p_out.at[step], p_in.at[3 - step], p_send.at[step - 1], p_recv.at[3 - step], {Z: near(2, step)}
        )
        copy.start()
        back_copies.append(copy)
    attend(7, 12)
    ring_pass(2)
    for copy in back_copies:
        copy.wait()

    n_chip = same(ids[chip], ids[chip + 4], 512.0)
    n_core = same(ids[chip + 3], ids[chip + 4], 0.0)
    mine = jnp.where(c == 1, n_core, FAR)
    theirs = jnp.where(c == 0, n_core, FAR)
    for step in range(4):
        for j in range(2):
            i = spots[step] * 2 + j
            rate = rates[c * 8 + i]
            part = slice(j * DH, j * DH + DH)
            before = (p_out[0, part, :] if step == 0 else p_in[step - 1, part, :]).astype(F32)
            own = before * decay(rate, jnp.where(c == 1, n_chip, 0.0)) + s_in[i] * decay(rate, mine)
            away = before * decay(rate, jnp.where(c == 0, n_chip, 0.0)) + s_own[i] * decay(rate, theirs)
            p_own[i] = own.astype(BF16)
            c_out[i] = away.astype(BF16)
    pair_copy = remote(c_out, c_in, d_send, d_recv, {C: 1 - c})
    pair_copy.start()
    attend(12, 16)

    def finish(first, ref):
        @pl.loop(0, 8)
        def _(i):
            h = first + i
            carried = dot(q[:, cols(h)], ref[i], 1, 0)
            mixed = inner[h] + carried * jnp.exp(-rates[h] * reach_n[...])
            mixed = mixed.astype(BF16).astype(F32)
            inv = lax.rsqrt(jnp.mean(mixed * mixed, axis=-1, keepdims=True) + 1e-06)
            nrm[:, cols(h)] = (mixed * inv * gated[h]).astype(BF16)

    def put(first, slot):
        half = pl.ds(pl.multiple_of(first * DH, 1024), 1024)
        return pltpu.make_async_copy(nrm.at[:, half], nrm_hbm.at[:, half], store_sem.at[slot])

    finish(c * 8, p_own)
    put(c * 8, 0).start()
    pair_copy.wait()
    finish((1 - c) * 8, c_in)
    put((1 - c) * 8, 1).start()

    ring_end(2)
    for where, slot in twins:
        twin_copy(where, slot).wait_recv()
    for copy in started:
        copy.wait_send()
    put(c * 8, 0).wait()
    put((1 - c) * 8, 1).wait()


def gather_and_attend(ids, rates, q, k, v, g, gain, w):
    tokens, width = q.shape
    heads = rates.shape[0]
    hbm = pl.BlockSpec(memory_space=pl.ANY)
    smem = pl.BlockSpec(memory_space=pltpu.SMEM)
    vmem = pltpu.VMEM
    dma = pltpu.SemaphoreType.DMA
    rows = w.shape[0]
    return pl.pallas_call(
        scan_kernel,
        out_shape=(
            jax.ShapeDtypeStruct((tokens, width), BF16),
            jax.ShapeDtypeStruct((4, 4, 4, 2, rows, width), BF16),
        ),
        in_specs=[smem, smem, hbm, hbm, hbm, hbm, pl.BlockSpec(memory_space=vmem), hbm],
        out_specs=(hbm, hbm),
        scratch_shapes=[
            vmem((tokens, width), BF16),
            vmem((tokens, width), BF16),
            vmem((tokens, width), BF16),
            vmem((tokens, width), BF16),
            vmem((rows, width), BF16),
            vmem((tokens, width), BF16),
            vmem((heads, tokens, DH), F32),
            vmem((heads, tokens, DH), F32),
            vmem((512, 256), F32),
            vmem((256, 256), F32),
            vmem((512, DH), F32),
            vmem((512, DH), F32),
            vmem((8, DH, DH), F32),
            vmem((8, DH, DH), F32),
            vmem((8, DH, DH), F32),
            vmem((4, 2 * DH, DH), BF16),
            vmem((3, 2 * DH, DH), BF16),
            vmem((4, 2 * DH, DH), F32),
            vmem((2 * DH + 8, DH), F32),
            vmem((3, 2 * DH + 8, DH), F32),
            vmem((2 * DH + 8, DH), F32),
            vmem((3, 2 * DH + 8, DH), F32),
            vmem((4, 2 * DH, DH), BF16),
            vmem((3, 2 * DH, DH), BF16),
            vmem((8, DH, DH), BF16),
            vmem((8, DH, DH), BF16),
            vmem((8, DH, DH), BF16),
            dma((5,)),
            dma((3,)),
            dma, dma,
            dma((3,)), dma((3,)),
            dma((3,)), dma((3,)),
            dma((3,)), dma((3,)),
            dma((3,)), dma((3,)),
            dma, dma,
            dma((3, 3, 6)), dma((3, 3, 6)),
            dma((28,)), dma((28,)),
        ],
        compiler_params=pltpu.CompilerParams(
            collective_id=0, has_side_effects=True, vmem_limit_bytes=60 << 20
        ),
        name="scan_and_gather",
    )(ids, rates, q, k, v, g, gain, w)


def on_device(query_rows, key_rows, value_rows, gate_rows, segment_ids, decay_rates, norm_gain, out_weight):
    width = query_rows.shape[1]
    normed, weight = gather_and_attend(
        segment_ids, decay_rates, query_rows, key_rows, value_rows, gate_rows,
        norm_gain.reshape(1, width), out_weight,
    )
    return jnp.dot(
        normed, weight.reshape(width, width), preferred_element_type=F32
    ).astype(BF16)


def solution(mesh):
    split = Mesh(mesh.devices.reshape(4, 4, 4, 2), SEQ_HEAD)
    rows = P(SEQ_HEAD, None)
    return jax.shard_map(
        on_device,
        mesh=split,
        in_specs=(rows, rows, rows, rows, P(SEQ), P(), P(), rows),
        out_specs=rows,
        check_vma=False,
    )
```

time: 353 us -> 69.5 us (0.20)
  waiting for transfers between devices: 155 us -> 0 us
  Pallas kernels: 0 us -> 59.6 us
  between operations: 57.5 us -> 0.01 us
  blocking collectives: 46.7 us -> 0 us
  matrix products: 40.8 us -> 9.84 us
  local copies, waits for them, and re-layouts: 25.8 us -> 0 us
  other arithmetic: 25.5 us -> 0 us
    all_gather x5 -> x0, waiting for transfers between devices: 155 us -> none  [the longest x4 102 us: prefix_by_axis(): pieces = jax.tree.map(lambda part: lax.all_gather(part, axis), subtotal)]
    pallas_call x0 -> x1, Pallas kernels: none -> 59.6 us  [gather_and_attend(): pl.pallas_call(scan_kernel, out_shape=(jax.ShapeDtypeStruct((tokens, widt...]
    dot_general x5 -> x1, matrix products: 40.8 us -> 9.84 us  [on_device(): jnp.dot(normed, weight.reshape(width, width), preferred_element_type=F32)]
    unnamed x4 -> x0, blocking collectives: 30.5 us -> none
    all_gather x2 -> x0, blocking collectives: 16.2 us -> none  [prefix_by_axis(): pieces = jax.tree.map(lambda part: lax.all_gather(part, axis), subtotal)]
    unnamed x26 -> x0, local copies, waits for them, and re-layouts: 15.2 us -> none
    add x3 -> x0, other arithmetic: 9.94 us -> none  [link_pieces(): state_both = state_late + factor[:, None, None] * state_early]
    select_n x15 -> x0, other arithmetic: 6.15 us -> none  [the longest x2 2.4 us: prefix_by_axis(): jnp.where(passed, new, old)]
  transfers between devices with their start and end apart: 5 -> 0, of which waited for: 5 -> 0; matrix products, arithmetic and copies ran while one was open for 10% -> 0% of each run, Pallas kernels for 0% -> 0%
where the time goes in v1:
time: 69.5 us; the launch traced here: 69.4 us
  Pallas kernels  59.6 us (86%)
  matrix products  9.84 us (14%)
    pallas_call x1, Pallas kernels, gather_and_attend(): pl.pallas_call(scan_kernel, out_shape=(jax.ShapeDtypeStruct((tokens, widt...  59.6 us
    dot_general x1, matrix products, on_device(): jnp.dot(normed, weight.reshape(width, width), preferred_element_type=F32)  9.84 us

profile of v1, /device:TPU:1, one launch (start us, length us, event | category | flops | bytes accessed | tf_op | source)
XLA Modules:
  0.0 69.4 jit_solution(10713200553898628131)
XLA Ops:
  0.0 59.6 %scan_and_gather.1 = (bf16[512,2048]{1,0:T(8,128)(2,1)}, bf16[4,4,4,2,16,2048]{5,4,3,2,1,0:T(8,128)(2,1)}) custom-call(s32[32]{0:T(128)} %ids.1, f32[16]{0:T(128)} %rates.1, bf16[512,2048]{1,0:T(8,128)(2,1)} %q_hbm.1, bf16[512,2048]{1,0:T(8,128)(2,1)} %k_hbm.1, bf16[512,2048]{1,0:T(8,128)(2,1)} %v_hbm.1, bf16[512,2048]{1,0:T(8,128)(2,1)} %g_hbm.1, ...), custom_call_target="tpu_custom_call" | custom-call | tf_op jit(solution)/shard_map/scan_and_gather/pallas_call | solution.py:402
  59.6 9.8 %convolution_convert_fusion = bf16[512,2048]{1,0:T(8,128)(2,1)} fusion(bf16[512,2048]{1,0:T(8,128)(2,1)} %get-tuple-element.7, bf16[2048,2048]{1,0:T(8,128)(2,1)} %bitcast.5), kind=kOutput, calls=%fused_computation | convolution fusion | flops 4296015872 | bytes 12582912 | tf_op jit(solution)/shard_map/dot_general | solution.py:462

commit v2 on v1

v2 whole, which is shorter than its diff:
```python
import functools

import jax
import jax.numpy as jnp
from jax import lax
from jax.experimental import pallas as pl
from jax.experimental.pallas import tpu as pltpu
from jax.sharding import Mesh
from jax.sharding import PartitionSpec as P

BLK = 128
SBLK = 512
DH = 128
FAR = 1e30
X, Y, Z, C = "seq_0", "seq_1", "head_0", "head_1"
SEQ_HEAD = (X, Y, Z, C)
SEQ = (X, Y)
MESH_ID = pl.DeviceIdType.MESH
F32, BF16 = jnp.float32, jnp.bfloat16

COLOURS = (
    (0, 768, (2, 1, 0)),
    (768, 640, (1, 0, 2)),
    (1408, 640, (0, 2, 1)),
)


def dot(a, b, ca, cb):
    return lax.dot_general(a, b, (((ca,), (cb,)), ((), ())), preferred_element_type=F32)


def same(a, b, n):
    return jnp.where(a == b, n, FAR)


def decay(rate, n):
    return jnp.exp(-rate * jnp.broadcast_to(n, (1, DH)))


def scan_kernel(
    ids, rates, q_hbm, k_hbm, v_hbm, g_hbm, gain, w_in,
    nrm_hbm, w_all,
    q, k, v, g, wbuf, nrm, inner, gated, offs0, offs1, keep_n, lasting, reach_n,
    s_own, s_out, s_in, z_out, z_in, p_part, y_out, y_in, x_out, x_in, u_out, u_in, m_out, m_in,
    p_out, p_in, c_out, c_in, p_own,
    load_sem, store_sem, c_send, c_recv, z_send, z_recv, y_send, y_recv, x_send, x_recv,
    u_send, u_recv, m_send, m_recv, p_send, p_recv, d_send, d_recv, w_send, w_recv, b_send, b_recv,
):
    at = (lax.axis_index(X), lax.axis_index(Y), lax.axis_index(Z))
    x, y, z = at
    c = lax.axis_index(C)
    names = (X, Y, Z)

    def near(axis, step):
        return lax.rem(at[axis] + step, 4)

    barrier = pltpu.get_barrier_semaphore()
    pl.semaphore_signal(barrier, inc=1, device_id={C: 1 - c}, device_id_type=MESH_ID)
    for axis in range(3):
        for step in (1, 2, 3):
            pl.semaphore_signal(
                barrier, inc=1, device_id={names[axis]: near(axis, step)}, device_id_type=MESH_ID
            )
    loads = [
        pltpu.make_async_copy(src, dst, load_sem.at[n])
        for n, (src, dst) in enumerate(
            ((w_in, wbuf), (k_hbm, k), (v_hbm, v), (q_hbm, q), (g_hbm, g))
        )
    ]
    for load in loads:
        load.start()

    place = z * 2 + c
    own_id = [ids[place * 4 + b] for b in range(4)]
    row = lax.broadcasted_iota(jnp.int32, (BLK, BLK), 0)
    column = lax.broadcasted_iota(jnp.int32, (BLK, BLK), 1)
    rows = row.astype(F32)
    ahead = (row - column).astype(F32)
    for bi in range(4):
        part = slice(bi * BLK, bi * BLK + BLK)
        keep_n[part, :] = (SBLK - 1.0 - bi * BLK) - rows + same(own_id[bi], own_id[3], 0.0)
        lasting[part, :] = jnp.full((BLK, DH), jnp.where(own_id[bi] == own_id[3], 1.0, 0.0), F32)
        reach_n[part, :] = (1.0 + bi * BLK) + rows + same(own_id[bi], own_id[0], 0.0)
        for bj in range(4):
            if bj >= 2 and bi < 2:
                continue
            if bj > bi:
                block = jnp.full((BLK, BLK), FAR, F32)
            else:
                block = ahead + float(BLK * (bi - bj))
                if bi == bj:
                    block = jnp.where(ahead >= 0, block, FAR)
                block = block + same(own_id[bi], own_id[bj], 0.0)
            if bj < 2:
                offs0[part, bj * BLK : bj * BLK + BLK] = block
            else:
                offs1[bi * BLK - 256 : bi * BLK - 128, bj * BLK - 256 : bj * BLK - 128] = block

    def cols(h):
        return pl.ds(pl.multiple_of(h * DH, DH), DH)

    def states(into, first):
        @pl.loop(0, 8)
        def _(i):
            h = first + i
            keys, values = k[:, cols(h)], v[:, cols(h)]
            lost = keys.astype(F32) * (lasting[...] - jnp.exp(-rates[h] * keep_n[...]))
            exact = keys * lasting[...].astype(BF16)
            into[i] = dot(exact, values, 0, 0) - dot(lost.astype(BF16), values, 0, 0)

    def attend(low, high):
        @pl.loop(low, high)
        def _(h):
            rate = rates[h]
            queries, keys, values = q[:, cols(h)], k[:, cols(h)], v[:, cols(h)]
            scores = dot(queries, keys[:256], 1, 1)
            weights = (scores * jnp.exp(-rate * offs0[...])).astype(BF16)
            total = dot(weights, values[:256], 1, 0)
            scores = dot(queries[256:], keys[256:], 1, 1)
            weights = (scores * jnp.exp(-rate * offs1[...])).astype(BF16)
            inner[h, :256, :] = total[:256]
            inner[h, 256:, :] = total[256:] + dot(weights, values[256:], 1, 0)
            gate = g[:, cols(h)].astype(F32)
            gated[h] = gain[:, cols(h)] * (gate / (1.0 + jnp.exp(-gate)))

    def remote(src, dst, send, recv, to):
        return pltpu.make_async_remote_copy(
            src_ref=src, dst_ref=dst, send_sem=send, recv_sem=recv, device_id=to, device_id_type=MESH_ID
        )

    SLOTS = ((1, 0), (1, 1), (3, 1), (3, 0), (1, 0), (3, 1))

    def phase_of(group):
        return min(group, 2)

    def piece(colour, group, coord, half):
        low, wide, order = COLOURS[colour]
        phase = phase_of(group)
        index = list(at) + [c]
        lanes = slice(low, low + wide)
        if phase == 0:
            if half is not None:
                lanes = slice(low, low + 384) if half == 0 else slice(low + 384, low + wide)
        else:
            index[order[0]] = slice(0, 4) if half is None else slice(2 * half, 2 * half + 2)
        if phase == 2:
            index[order[1]] = near(order[1], group - 2)
        index[order[phase]] = coord
        return tuple(index) + (slice(None), lanes)

    started = []

    def ring_copy(colour, group, slot, step, coord, half):
        axis = COLOURS[colour][2][phase_of(group)]
        where = piece(colour, group, coord, half)
        src = w_all.at[where]
        if group == 0 and slot < 4:
            src = wbuf.at[where[-2:]]
        return remote(
            src, w_all.at[where], w_send.at[colour, group, slot], w_recv.at[colour, group, slot],
            {names[axis]: near(axis, step)},
        )

    def ring_start(group):
        for colour in range(3):
            mine = at[COLOURS[colour][2][phase_of(group)]]
            for slot in (0, 2, 1, 3):
                step, half = SLOTS[slot]
                copy = ring_copy(colour, group, slot, step, mine, half)
                copy.start()
                started.append(copy)

    def ring_pass(group):
        for colour in range(3):
            axis = COLOURS[colour][2][phase_of(group)]
            for slot in (0, 2):
                step, half = SLOTS[slot]
                from_coord = near(axis, 4 - step)
                ring_copy(colour, group, slot, step, from_coord, half).wait_recv()
                copy = ring_copy(colour, group, 4 if slot == 0 else 5, step, from_coord, half)
                copy.start()
                started.append(copy)

    twins = []

    def twin(where, slot):
        copy = remote(w_all.at[where], w_all.at[where], b_send.at[slot], b_recv.at[slot], {C: 1 - c})
        copy.start()
        started.append(copy)
        twins.append((where[:3] + (1 - c,) + where[4:], slot))

    def ring_end(group):
        for colour in range(3):
            axis = COLOURS[colour][2][phase_of(group)]
            for slot in (1, 3):
                step, half = SLOTS[slot]
                ring_copy(colour, group, slot, step, near(axis, 4 - step), half).wait_recv()
            if group > 0:
                twin(piece(colour, group, near(axis, 1), None), 18 * colour + 3 * group)
                twin(piece(colour, group, near(axis, 3), None), 18 * colour + 3 * group + 1)
        for colour in range(3):
            axis = COLOURS[colour][2][phase_of(group)]
            for slot in (4, 5):
                step, half = SLOTS[slot]
                ring_copy(colour, group, slot, step, near(axis, 2), half).wait_recv()
            if group == 0:
                twin(piece(colour, 1, at[COLOURS[colour][2][1]], None), 18 * colour)
            else:
                twin(piece(colour, group, near(axis, 2), None), 18 * colour + 3 * group + 2)

    def twin_waits():
        for where, slot in twins:
            view = w_all.at[where]
            remote(view, view, b_send.at[slot], b_recv.at[slot], {C: 1 - c}).wait_recv()

    pl.semaphore_wait(barrier, 10)
    loads[0].wait()
    ring_start(0)
    own_store = pltpu.make_async_copy(wbuf, w_all.at[x, y, z, c], store_sem.at[2])
    own_store.start()
    loads[1].wait()
    loads[2].wait()
    states(s_out, (1 - c) * 8)
    core_copy = remote(s_out, s_in, c_send, c_recv, {C: 1 - c})
    core_copy.start()
    states(s_own, c * 8)
    core_copy.wait()

    chip = z * 8
    n_first = jnp.where(c == 0, same(ids[chip + 3], ids[chip + 7], 512.0), 0.0)
    n_second = jnp.where(c == 1, same(ids[chip + 3], ids[chip + 7], 512.0), 0.0)
    for i in range(8):
        rate = rates[c * 8 + i]
        both = s_own[i] * decay(rate, n_first) + s_in[i] * decay(rate, n_second)
        z_out[i // 2, (i % 2) * DH : (i % 2) * DH + DH, :] = both.astype(BF16)

    def spread(copies):
        for copy in copies:
            copy.start()
        return copies

    def settle(copies):
        for copy in copies:
            copy.wait()

    line_copies = spread([
        remote(
            z_out.at[near(2, step)], z_in.at[3 - step], z_send.at[step - 1], z_recv.at[3 - step],
            {Z: near(2, step)},
        )
        for step in (1, 3, 2)
    ])
    loads[3].wait()
    loads[4].wait()
    ring_pass(0)
    attend(0, 1)
    own_store.wait()
    ring_end(0)
    ring_start(1)
    ring_start(2)
    attend(1, 4)
    ring_pass(1)
    attend(4, 5)
    settle(line_copies)

    two = [rates[c * 8 + z * 2 + j] for j in range(2)]
    spots = [near(2, step) for step in range(4)]
    line_first, line_last = ids[0], ids[31]
    halves = (slice(0, DH), slice(DH, 2 * DH))

    def held(step, j):
        block = z_out[z, halves[j], :] if step == 0 else z_in[step - 1, halves[j], :]
        return block.astype(F32)

    for j, out in enumerate((y_out, x_out)):
        total = None
        for step in range(4):
            spot = spots[step]
            n = same(ids[spot * 8 + 7], line_last, (1024 * (3 - spot)).astype(F32))
            term = held(step, j) * decay(two[j], n)
            total = term if total is None else total + term
        out[:DH, :] = total.astype(BF16)
        note_row = lax.broadcasted_iota(jnp.int32, (16, DH), 0)
        notes = jnp.where(note_row < 8, line_last.astype(F32), line_first.astype(F32))
        out[DH : DH + 16, :] = notes.astype(BF16)
    column_copies = spread(
        [
            remote(
                src, into.at[3 - step], send.at[step - 1], recv.at[3 - step],
                {names[axis]: near(axis, step)},
            )
            for step in (1, 3, 2)
            for axis, src, into, send, recv in (
                (1, y_out, y_in, y_send, y_recv), (0, x_out, x_in, x_send, x_recv),
            )
        ]
    )
    for t in range(4):
        target = spots[t]
        for j in range(2):
            total = None
            for step in range(4):
                if step == t:
                    continue
                spot = spots[step]
                n = same(ids[spot * 8 + 7], ids[target * 8], (1024 * (target - 1 - spot)).astype(F32))
                term = held(step, j) * decay(two[j], jnp.where(spot < target, n, FAR))
                total = term if total is None else total + term
            p_part[t, halves[j], :] = total
    ring_end(1)
    for group in (3, 5, 4):
        ring_start(group)
    ring_pass(2)
    attend(5, 8)
    settle(column_copies)

    spots_y = [near(1, step) for step in range(4)]
    spots_x = [near(0, step) for step in range(4)]

    def view(own, came, step):
        return own if step == 0 else came.at[step - 1]

    def body_of(ref):
        return ref[:DH, :].astype(F32)

    def last_of(ref):
        return ref[DH : DH + 1, :].astype(F32)

    def first_of(ref):
        return ref[DH + 8 : DH + 9, :].astype(F32)

    by_y = [view(y_out, y_in, step) for step in range(4)]
    by_x = [view(x_out, x_in, step) for step in range(4)]
    slab_last = jnp.zeros((1, DH), F32)
    for step in range(4):
        slab_last = slab_last + jnp.where(spots_y[step] == 3, 1.0, 0.0) * last_of(by_y[step])
    total = None
    for step in range(4):
        spot = spots_y[step]
        n = same(last_of(by_y[step]), slab_last, (4096 * (3 - spot)).astype(F32))
        term = body_of(by_y[step]) * decay(two[0], n)
        total = term if total is None else total + term
    u_out[:DH, :] = total.astype(BF16)
    u_out[DH : DH + 16, :] = jnp.broadcast_to(slab_last, (16, DH)).astype(BF16)
    for t in range(4):
        target, first = spots_y[t], first_of(by_y[t])
        total = None
        for step in range(4):
            ref = by_x[step]
            if step == 0:
                n = same(last_of(ref), first, (4096 * (target - 1 - y)).astype(F32))
                n = jnp.where(y < target, n, FAR)
            else:
                spot = spots_x[step]
                lines = 4 * (x - spot) - y - 1 + target
                n = same(last_of(ref), first, (4096 * lines).astype(F32))
                n = jnp.where(spot < x, n, FAR)
            term = body_of(ref) * decay(two[1], n)
            total = term if total is None else total + term
        m_out[t] = total.astype(BF16)
    slab_copies = spread(
        [
            copy
            for step in (1, 3, 2)
            for copy in (
                remote(
                    u_out, u_in.at[3 - step], u_send.at[step - 1], u_recv.at[3 - step],
                    {X: near(0, step)},
                ),
                remote(
                    m_out.at[step], m_in.at[3 - step], m_send.at[step - 1], m_recv.at[3 - step],
                    {Y: near(1, step)},
                ),
            )
        ]
    )
    attend(8, 9)
    ring_end(2)
    ring_pass(3)
    attend(9, 11)
    settle(slab_copies)

    total = jnp.zeros((DH, DH), F32)
    first = line_first.astype(F32)
    for step in range(1, 4):
        ref, spot = by_y[step], spots_y[step]
        n = same(last_of(ref), first, (4096 * (y - 1 - spot)).astype(F32))
        total = total + body_of(ref) * decay(two[0], jnp.where(spot < y, n, FAR))
        ref, spot = u_in.at[step - 1], spots_x[step]
        n = same(last_of(ref), first, (16384 * (x - 1 - spot) + 4096 * y).astype(F32))
        total = total + body_of(ref) * decay(two[0], jnp.where(spot < x, n, FAR))
    fronts = [total]
    total = m_out[0].astype(F32)
    for step in range(3):
        total = total + m_in[step].astype(F32)
    fronts.append(total)
    for t in range(4):
        n = same(line_first, ids[spots[t] * 8], (1024 * spots[t]).astype(F32))
        for j in range(2):
            whole = p_part[t, halves[j], :] + fronts[j] * decay(two[j], n)
            p_out[t, halves[j], :] = whole.astype(BF16)
    back_copies = spread([
        remote(
            p_out.at[step], p_in.at[3 - step], p_send.at[step - 1], p_recv.at[3 - step],
            {Z: near(2, step)},
        )
        for step in (1, 3, 2)
    ])
    ring_pass(5)
    attend(11, 13)
    ring_pass(4)
    attend(13, 15)
    settle(back_copies)

    n_chip = same(ids[chip], ids[chip + 4], 512.0)
    n_core = same(ids[chip + 3], ids[chip + 4], 0.0)
    mine = jnp.where(c == 1, n_core, FAR)
    theirs = jnp.where(c == 0, n_core, FAR)
    for step in range(4):
        for j in range(2):
            i = spots[step] * 2 + j
            rate = rates[c * 8 + i]
            before = (p_out[0, halves[j], :] if step == 0 else p_in[step - 1, halves[j], :]).astype(F32)
            own = before * decay(rate, jnp.where(c == 1, n_chip, 0.0)) + s_in[i] * decay(rate, mine)
            away = before * decay(rate, jnp.where(c == 0, n_chip, 0.0)) + s_own[i] * decay(rate, theirs)
            p_own[i] = own.astype(BF16)
            c_out[i] = away.astype(BF16)
    pair_copy = remote(c_out, c_in, d_send, d_recv, {C: 1 - c})
    pair_copy.start()
    attend(15, 16)
    ring_end(3)

    def finish(first, ref):
        @pl.loop(0, 8)
        def _(i):
            h = first + i
            carried = dot(q[:, cols(h)], ref[i], 1, 0)
            mixed = inner[h] + carried * jnp.exp(-rates[h] * reach_n[...])
            mixed = mixed.astype(BF16).astype(F32)
            inv = lax.rsqrt(jnp.mean(mixed * mixed, axis=-1, keepdims=True) + 1e-06)
            nrm[:, cols(h)] = (mixed * inv * gated[h]).astype(BF16)

    def put(first, slot):
        half = pl.ds(pl.multiple_of(first * DH, 1024), 1024)
        return pltpu.make_async_copy(nrm.at[:, half], nrm_hbm.at[:, half], store_sem.at[slot])

    finish(c * 8, p_own)
    put(c * 8, 0).start()
    ring_end(5)
    ring_end(4)
    pair_copy.wait()
    finish((1 - c) * 8, c_in)
    put((1 - c) * 8, 1).start()
    twin_waits()
    for copy in started:
        copy.wait_send()
    put(c * 8, 0).wait()
    put((1 - c) * 8, 1).wait()


def gather_and_attend(ids, rates, q, k, v, g, gain, w):
    tokens, width = q.shape
    heads = rates.shape[0]
    hbm = pl.BlockSpec(memory_space=pl.ANY)
    smem = pl.BlockSpec(memory_space=pltpu.SMEM)
    vmem = pltpu.VMEM
    dma = pltpu.SemaphoreType.DMA
    rows = w.shape[0]
    return pl.pallas_call(
        scan_kernel,
        out_shape=(
            jax.ShapeDtypeStruct((tokens, width), BF16),
            jax.ShapeDtypeStruct((4, 4, 4, 2, rows, width), BF16),
        ),
        in_specs=[smem, smem, hbm, hbm, hbm, hbm, pl.BlockSpec(memory_space=vmem), hbm],
        out_specs=(hbm, hbm),
        scratch_shapes=[
            vmem((tokens, width), BF16),
            vmem((tokens, width), BF16),
            vmem((tokens, width), BF16),
            vmem((tokens, width), BF16),
            vmem((rows, width), BF16),
            vmem((tokens, width), BF16),
            vmem((heads, tokens, DH), F32),
            vmem((heads, tokens, DH), F32),
            vmem((512, 256), F32),
            vmem((256, 256), F32),
            vmem((512, DH), F32),
            vmem((512, DH), F32),
            vmem((512, DH), F32),
            vmem((8, DH, DH), F32),
            vmem((8, DH, DH), F32),
            vmem((8, DH, DH), F32),
            vmem((4, 2 * DH, DH), BF16),
            vmem((3, 2 * DH, DH), BF16),
            vmem((4, 2 * DH, DH), F32),
            vmem((DH + 16, DH), BF16),
            vmem((3, DH + 16, DH), BF16),
            vmem((DH + 16, DH), BF16),
            vmem((3, DH + 16, DH), BF16),
            vmem((DH + 16, DH), BF16),
            vmem((3, DH + 16, DH), BF16),
            vmem((4, DH, DH), BF16),
            vmem((3, DH, DH), BF16),
            vmem((4, 2 * DH, DH), BF16),
            vmem((3, 2 * DH, DH), BF16),
            vmem((8, DH, DH), BF16),
            vmem((8, DH, DH), BF16),
            vmem((8, DH, DH), BF16),
            dma((5,)),
            dma((3,)),
            dma, dma,
            dma((3,)), dma((3,)),
            dma((3,)), dma((3,)),
            dma((3,)), dma((3,)),
            dma((3,)), dma((3,)),
            dma((3,)), dma((3,)),
            dma((3,)), dma((3,)),
            dma, dma,
            dma((3, 6, 6)), dma((3, 6, 6)),
            dma((54,)), dma((54,)),
        ],
        compiler_params=pltpu.CompilerParams(
            collective_id=0, has_side_effects=True, vmem_limit_bytes=60 << 20
        ),
        name="scan_and_gather",
    )(ids, rates, q, k, v, g, gain, w)


def project_kernel(a, b, o):
    o[...] = jnp.dot(a[...], b[...], preferred_element_type=F32).astype(BF16)


def project(a, b):
    rows, depth = a.shape
    columns = b.shape[1]
    tile = 1024
    return pl.pallas_call(
        project_kernel,
        out_shape=jax.ShapeDtypeStruct((rows, columns), BF16),
        grid=(columns // tile,),
        in_specs=[
            pl.BlockSpec((rows, depth), lambda j: (0, 0)),
            pl.BlockSpec((depth, tile), lambda j: (0, j)),
        ],
        out_specs=pl.BlockSpec((rows, tile), lambda j: (0, j)),
        compiler_params=pltpu.CompilerParams(vmem_limit_bytes=60 << 20),
        name="project",
    )(a, b)


def on_device(query_rows, key_rows, value_rows, gate_rows, segment_ids, decay_rates, norm_gain, out_weight):
    width = query_rows.shape[1]
    normed, weight = gather_and_attend(
        segment_ids, decay_rates, query_rows, key_rows, value_rows, gate_rows,
        norm_gain.reshape(1, width), out_weight,
    )
    return project(normed, weight.reshape(width, width))


def solution(mesh):
    split = Mesh(mesh.devices.reshape(4, 4, 4, 2), SEQ_HEAD)
    rows = P(SEQ_HEAD, None)
    return jax.shard_map(
        on_device,
        mesh=split,
        in_specs=(rows, rows, rows, rows, P(SEQ), P(), P(), rows),
        out_specs=rows,
        check_vma=False,
    )
```

time: 69.5 us -> 63.2 us (0.909)
  matrix products: 9.84 us -> 0 us
  Pallas kernels: 59.6 us -> 63 us
    dot_general x1 -> x0, matrix products: 9.84 us -> none  [on_device(): jnp.dot(normed, weight.reshape(width, width), preferred_element_type=F32)]
    pallas_call x0 -> x1, Pallas kernels: none -> 8.53 us  [project(): pl.pallas_call(project_kernel, out_shape=jax.ShapeDtypeStruct((rows, colu...]
    pallas_call x1, Pallas kernels: 59.6 us -> 54.5 us  [gather_and_attend(): pl.pallas_call(scan_kernel, out_shape=(jax.ShapeDtypeStruct((tokens, widt...]
where the time goes in v2:
time: 63.2 us; the launch traced here: 63 us
  Pallas kernels  63 us (100%)
    pallas_call x1, Pallas kernels, gather_and_attend(): pl.pallas_call(scan_kernel, out_shape=(jax.ShapeDtypeStruct((tokens, widt...  54.5 us
    pallas_call x1, Pallas kernels, project(): pl.pallas_call(project_kernel, out_shape=jax.ShapeDtypeStruct((rows, colu...  8.53 us

profile of v2, /device:TPU:1, one launch (start us, length us, event | category | flops | bytes accessed | tf_op | source)
XLA Modules:
  0.0 63.0 jit_solution(8211052345528801732)
XLA Ops:
  0.0 54.5 %scan_and_gather.1 = (bf16[512,2048]{1,0:T(8,128)(2,1)}, bf16[4,4,4,2,16,2048]{5,4,3,2,1,0:T(8,128)(2,1)}) custom-call(s32[32]{0:T(128)} %ids.1, f32[16]{0:T(128)} %rates.1, bf16[512,2048]{1,0:T(8,128)(2,1)} %q_hbm.1, bf16[512,2048]{1,0:T(8,128)(2,1)} %k_hbm.1, bf16[512,2048]{1,0:T(8,128)(2,1)} %v_hbm.1, bf16[512,2048]{1,0:T(8,128)(2,1)} %g_hbm.1, ...), custom_call_target="tpu_custom_call" | custom-call | tf_op jit(solution)/shard_map/scan_and_gather/pallas_call | solution.py:469
  54.5 8.5 %project.1 = bf16[512,2048]{1,0:T(8,128)(2,1)} custom-call(bf16[512,2048]{1,0:T(8,128)(2,1)} %get-tuple-element.7.a, bf16[2048,2048]{1,0:T(8,128)(2,1)} %bitcast.2), custom_call_target="tpu_custom_call" | custom-call | tf_op jit(solution)/shard_map/project/pallas_call | solution.py:538

commit v3 on v2

--- a/solution.py
+++ b/solution.py
@@ -40,7 +40,7 @@
 def scan_kernel(
     ids, rates, q_hbm, k_hbm, v_hbm, g_hbm, gain, w_in,
     nrm_hbm, w_all,
-    q, k, v, g, wbuf, nrm, inner, gated, offs0, offs1, keep_n, lasting, reach_n,
+    q, k, v, g, wbuf, nrm, inner, gated, keep_n, lasting,
     s_own, s_out, s_in, z_out, z_in, p_part, y_out, y_in, x_out, x_in, u_out, u_in, m_out, m_in,
     p_out, p_in, c_out, c_in, p_own,
     load_sem, store_sem, c_send, c_recv, z_send, z_recv, y_send, y_recv, x_send, x_recv,
@@ -74,27 +74,11 @@
     own_id = [ids[place * 4 + b] for b in range(4)]
     row = lax.broadcasted_iota(jnp.int32, (BLK, BLK), 0)
     column = lax.broadcasted_iota(jnp.int32, (BLK, BLK), 1)
-    rows = row.astype(F32)
-    ahead = (row - column).astype(F32)
-    for bi in range(4):
-        part = slice(bi * BLK, bi * BLK + BLK)
-        keep_n[part, :] = (SBLK - 1.0 - bi * BLK) - rows + same(own_id[bi], own_id[3], 0.0)
-        lasting[part, :] = jnp.full((BLK, DH), jnp.where(own_id[bi] == own_id[3], 1.0, 0.0), F32)
-        reach_n[part, :] = (1.0 + bi * BLK) + rows + same(own_id[bi], own_id[0], 0.0)
-        for bj in range(4):
-            if bj >= 2 and bi < 2:
-                continue
-            if bj > bi:
-                block = jnp.full((BLK, BLK), FAR, F32)
-            else:
-                block = ahead + float(BLK * (bi - bj))
-                if bi == bj:
-                    block = jnp.where(ahead >= 0, block, FAR)
-                block = block + same(own_id[bi], own_id[bj], 0.0)
-            if bj < 2:
-                offs0[part, bj * BLK : bj * BLK + BLK] = block
-            else:
-                offs1[bi * BLK - 256 : bi * BLK - 128, bj * BLK - 256 : bj * BLK - 128] = block
+    for b in range(4):
+        part = slice(b * BLK, b * BLK + BLK)
+        keep_n[part, :] = (SBLK - 1.0 - b * BLK) - row.astype(F32) + same(own_id[b], own_id[3], 0.0)
+        last = jnp.where(own_id[b] == own_id[3], 1.0, 0.0)
+        lasting[part, :] = jnp.full((BLK, DH), last, F32).astype(BF16)
 
     def cols(h):
         return pl.ds(pl.multiple_of(h * DH, DH), DH)
@@ -103,23 +87,51 @@
         @pl.loop(0, 8)
         def _(i):
             h = first + i
-            keys, values = k[:, cols(h)], v[:, cols(h)]
-            lost = keys.astype(F32) * (lasting[...] - jnp.exp(-rates[h] * keep_n[...]))
-            exact = keys * lasting[...].astype(BF16)
-            into[i] = dot(exact, values, 0, 0) - dot(lost.astype(BF16), values, 0, 0)
+            values = v[:, cols(h)]
+            lost = lasting[...].astype(F32) - jnp.exp(-rates[h] * keep_n[...])
+            pair = jnp.concatenate([values * lasting[...], values * lost.astype(BF16)], axis=1)
+            both = dot(k[:, cols(h)], pair, 0, 0)
+            into[i] = both[:, :DH] - both[:, DH:]
 
     def attend(low, high):
         @pl.loop(low, high)
         def _(h):
             rate = rates[h]
             queries, keys, values = q[:, cols(h)], k[:, cols(h)], v[:, cols(h)]
-            scores = dot(queries, keys[:256], 1, 1)
-            weights = (scores * jnp.exp(-rate * offs0[...])).astype(BF16)
-            total = dot(weights, values[:256], 1, 0)
-            scores = dot(queries[256:], keys[256:], 1, 1)
-            weights = (scores * jnp.exp(-rate * offs1[...])).astype(BF16)
+            ahead = row - column
+            base = jnp.exp(-rate * ahead.astype(F32))
+
+            def weigh(scores, bi, bj):
+                if bj > bi:
+                    return jnp.zeros((BLK, BLK), BF16)
+                table = jnp.where(ahead >= 0, base, 0.0) if bi == bj else base
+                n = same(own_id[bi], own_id[bj], float(BLK * (bi - bj)))
+                return (scores * (table * decay(rate, n))).astype(BF16)
+
+            for low_block in (0, 2):
+                first = low_block * BLK
+                scores = dot(queries[first:], keys[first : first + 256], 1, 1)
+                weights = jnp.concatenate(
+                    [
+                        jnp.concatenate(
+                            [
+                                weigh(
+                                    scores[bi * BLK - first : bi * BLK - first + BLK, j * BLK : j * BLK + BLK],
+                                    bi, low_block + j,
+                                )
+                                for j in range(2)
+                            ],
+                            axis=1,
+                        )
+                        for bi in range(low_block, 4)
+                    ],
+                    axis=0,
+                )
+                part = dot(weights, values[first : first + 256], 1, 0)
+                if low_block == 0:
+                    total = part
             inner[h, :256, :] = total[:256]
-            inner[h, 256:, :] = total[256:] + dot(weights, values[256:], 1, 0)
+            inner[h, 256:, :] = total[256:] + part
             gate = g[:, cols(h)].astype(F32)
             gated[h] = gain[:, cols(h)] * (gate / (1.0 + jnp.exp(-gate)))
 
@@ -138,11 +150,7 @@
         phase = phase_of(group)
         index = list(at) + [c]
         lanes = slice(low, low + wide)
-        if phase == 0:
-            if half is not None:
-                lanes = slice(low, low + 384) if half == 0 else slice(low + 384, low + wide)
-        else:
-            index[order[0]] = slice(0, 4) if half is None else slice(2 * half, 2 * half + 2)
+        index[order[0]] = slice(0, 4) if half is None else slice(2 * half, 2 * half + 2)
         if phase == 2:
             index[order[1]] = near(order[1], group - 2)
         index[order[phase]] = coord
@@ -153,13 +161,34 @@
     def ring_copy(colour, group, slot, step, coord, half):
         axis = COLOURS[colour][2][phase_of(group)]
         where = piece(colour, group, coord, half)
-        src = w_all.at[where]
-        if group == 0 and slot < 4:
-            src = wbuf.at[where[-2:]]
         return remote(
-            src, w_all.at[where], w_send.at[colour, group, slot], w_recv.at[colour, group, slot],
+            w_all.at[where], w_all.at[where], w_send.at[colour, group, slot], w_recv.at[colour, group, slot],
             {names[axis]: near(axis, step)},
         )
+
+    def direct_copy(colour, step, coord):
+        low, wide, order = COLOURS[colour]
+        index = list(at) + [c]
+        index[order[0]] = coord
+        return remote(
+            wbuf.at[:, low : low + wide], w_all.at[tuple(index) + (slice(None), slice(low, low + wide))],
+            w_send.at[colour, 0, step], w_recv.at[colour, 0, step], {names[order[0]]: near(order[0], step)},
+        )
+
+    def line_start():
+        for colour in range(3):
+            for step in (1, 3, 2):
+                copy = direct_copy(colour, step, at[COLOURS[colour][2][0]])
+                copy.start()
+                started.append(copy)
+
+    def line_end():
+        for colour in range(3):
+            axis = COLOURS[colour][2][0]
+            for step in (1, 3, 2):
+                direct_copy(colour, step, near(axis, 4 - step)).wait_recv()
+        for colour in range(3):
+            twin(piece(colour, 1, at[COLOURS[colour][2][1]], None), 18 * colour)
 
     def ring_start(group):
         for colour in range(3):
@@ -195,18 +224,14 @@
             for slot in (1, 3):
                 step, half = SLOTS[slot]
                 ring_copy(colour, group, slot, step, near(axis, 4 - step), half).wait_recv()
-            if group > 0:
-                twin(piece(colour, group, near(axis, 1), None), 18 * colour + 3 * group)
-                twin(piece(colour, group, near(axis, 3), None), 18 * colour + 3 * group + 1)
+            twin(piece(colour, group, near(axis, 1), None), 18 * colour + 3 * group)
+            twin(piece(colour, group, near(axis, 3), None), 18 * colour + 3 * group + 1)
         for colour in range(3):
             axis = COLOURS[colour][2][phase_of(group)]
             for slot in (4, 5):
                 step, half = SLOTS[slot]
                 ring_copy(colour, group, slot, step, near(axis, 2), half).wait_recv()
-            if group == 0:
-                twin(piece(colour, 1, at[COLOURS[colour][2][1]], None), 18 * colour)
-            else:
-                twin(piece(colour, group, near(axis, 2), None), 18 * colour + 3 * group + 2)
+            twin(piece(colour, group, near(axis, 2), None), 18 * colour + 3 * group + 2)
 
     def twin_waits():
         for where, slot in twins:
@@ -215,7 +240,7 @@
 
     pl.semaphore_wait(barrier, 10)
     loads[0].wait()
-    ring_start(0)
+    line_start()
     own_store = pltpu.make_async_copy(wbuf, w_all.at[x, y, z, c], store_sem.at[2])
     own_store.start()
     loads[1].wait()
@@ -252,15 +277,13 @@
     ])
     loads[3].wait()
     loads[4].wait()
-    ring_pass(0)
-    attend(0, 1)
     own_store.wait()
-    ring_end(0)
+    line_end()
     ring_start(1)
+    attend(0, 2)
+    ring_pass(1)
     ring_start(2)
-    attend(1, 4)
-    ring_pass(1)
-    attend(4, 5)
+    attend(2, 5)
     settle(line_copies)
 
     two = [rates[c * 8 + z * 2 + j] for j in range(2)]
@@ -308,8 +331,7 @@
                 total = term if total is None else total + term
             p_part[t, halves[j], :] = total
     ring_end(1)
-    for group in (3, 5, 4):
-        ring_start(group)
+    ring_start(3)
     ring_pass(2)
     attend(5, 8)
     settle(column_copies)
@@ -374,10 +396,10 @@
             )
         ]
     )
-    attend(8, 9)
     ring_end(2)
+    ring_start(5)
     ring_pass(3)
-    attend(9, 11)
+    attend(8, 11)
     settle(slab_copies)
 
     total = jnp.zeros((DH, DH), F32)
@@ -406,10 +428,10 @@
         )
         for step in (1, 3, 2)
     ])
+    ring_end(3)
+    ring_start(4)
     ring_pass(5)
-    attend(11, 13)
-    ring_pass(4)
-    attend(13, 15)
+    attend(11, 16)
     settle(back_copies)
 
     n_chip = same(ids[chip], ids[chip + 4], 512.0)
@@ -427,18 +449,20 @@
             c_out[i] = away.astype(BF16)
     pair_copy = remote(c_out, c_in, d_send, d_recv, {C: 1 - c})
     pair_copy.start()
-    attend(15, 16)
-    ring_end(3)
+    ring_pass(4)
 
     def finish(first, ref):
         @pl.loop(0, 8)
         def _(i):
             h = first + i
             carried = dot(q[:, cols(h)], ref[i], 1, 0)
-            mixed = inner[h] + carried * jnp.exp(-rates[h] * reach_n[...])
-            mixed = mixed.astype(BF16).astype(F32)
-            inv = lax.rsqrt(jnp.mean(mixed * mixed, axis=-1, keepdims=True) + 1e-06)
-            nrm[:, cols(h)] = (mixed * inv * gated[h]).astype(BF16)
+            base = jnp.exp(-rates[h] * (row.astype(F32) + 1.0))
+            for b in range(4):
+                part = slice(b * BLK, b * BLK + BLK)
+                reach = base * decay(rates[h], same(own_id[b], own_id[0], float(b * BLK)))
+                mixed = (inner[h, part, :] + carried[part] * reach).astype(BF16).astype(F32)
+                inv = lax.rsqrt(jnp.mean(mixed * mixed, axis=-1, keepdims=True) + 1e-06)
+                nrm[part, cols(h)] = (mixed * inv * gated[h, part, :]).astype(BF16)
 
     def put(first, slot):
         half = pl.ds(pl.multiple_of(first * DH, 1024), 1024)
@@ -483,11 +507,8 @@
             vmem((tokens, width), BF16),
             vmem((heads, tokens, DH), F32),
             vmem((heads, tokens, DH), F32),
-            vmem((512, 256), F32),
-            vmem((256, 256), F32),
             vmem((512, DH), F32),
-            vmem((512, DH), F32),
-            vmem((512, DH), F32),
+            vmem((512, DH), BF16),
             vmem((8, DH, DH), F32),
             vmem((8, DH, DH), F32),
             vmem((8, DH, DH), F32),

time: 63.2 us -> 57.7 us (0.913)
  Pallas kernels: 63 us -> 57.5 us
    pallas_call x1, Pallas kernels: 54.5 us -> 49 us  [gather_and_attend(): pl.pallas_call(scan_kernel, out_shape=(jax.ShapeDtypeStruct((tokens, widt...]
where the time goes in v3:
time: 57.7 us; the launch traced here: 57.5 us
  Pallas kernels  57.5 us (100%)
    pallas_call x1, Pallas kernels, gather_and_attend(): pl.pallas_call(scan_kernel, out_shape=(jax.ShapeDtypeStruct((tokens, widt...  49 us
    pallas_call x1, Pallas kernels, project(): pl.pallas_call(project_kernel, out_shape=jax.ShapeDtypeStruct((rows, colu...  8.53 us

profile of v3, /device:TPU:1, one launch (start us, length us, event | category | flops | bytes accessed | tf_op | source)
XLA Modules:
  0.0 57.5 jit_solution(758128878251735221)
XLA Ops:
  0.0 49.0 %scan_and_gather.1 = (bf16[512,2048]{1,0:T(8,128)(2,1)}, bf16[4,4,4,2,16,2048]{5,4,3,2,1,0:T(8,128)(2,1)}) custom-call(s32[32]{0:T(128)} %ids.1, f32[16]{0:T(128)} %rates.1, bf16[512,2048]{1,0:T(8,128)(2,1)} %q_hbm.1, bf16[512,2048]{1,0:T(8,128)(2,1)} %k_hbm.1, bf16[512,2048]{1,0:T(8,128)(2,1)} %v_hbm.1, bf16[512,2048]{1,0:T(8,128)(2,1)} %g_hbm.1, ...), custom_call_target="tpu_custom_call" | custom-call | tf_op jit(solution)/shard_map/scan_and_gather/pallas_call | solution.py:493
  49.0 8.5 %project.1 = bf16[512,2048]{1,0:T(8,128)(2,1)} custom-call(bf16[512,2048]{1,0:T(8,128)(2,1)} %get-tuple-element.7.a, bf16[2048,2048]{1,0:T(8,128)(2,1)} %bitcast.2), custom_call_target="tpu_custom_call" | custom-call | tf_op jit(solution)/shard_map/project/pallas_call | solution.py:559

commit v4 on v3

--- a/solution.py
+++ b/solution.py
@@ -20,8 +20,8 @@
 
 COLOURS = (
     (0, 768, (2, 1, 0)),
-    (768, 640, (1, 0, 2)),
-    (1408, 640, (0, 2, 1)),
+    (768, 512, (1, 0, 2)),
+    (1280, 768, (0, 2, 1)),
 )
 
 
@@ -39,8 +39,8 @@
 
 def scan_kernel(
     ids, rates, q_hbm, k_hbm, v_hbm, g_hbm, gain, w_in,
-    nrm_hbm, w_all,
-    q, k, v, g, wbuf, nrm, inner, gated, keep_n, lasting,
+    out_hbm,
+    q, k, v, g, w_all, nrm, mixed_out, inner, gated, keep_n, lasting,
     s_own, s_out, s_in, z_out, z_in, p_part, y_out, y_in, x_out, x_in, u_out, u_in, m_out, m_in,
     p_out, p_in, c_out, c_in, p_own,
     load_sem, store_sem, c_send, c_recv, z_send, z_recv, y_send, y_recv, x_send, x_recv,
@@ -64,7 +64,7 @@
     loads = [
         pltpu.make_async_copy(src, dst, load_sem.at[n])
         for n, (src, dst) in enumerate(
-            ((w_in, wbuf), (k_hbm, k), (v_hbm, v), (q_hbm, q), (g_hbm, g))
+            ((w_in, w_all.at[x, y, z, c]), (k_hbm, k), (v_hbm, v), (q_hbm, q), (g_hbm, g))
         )
     ]
     for load in loads:
@@ -84,7 +84,7 @@
         return pl.ds(pl.multiple_of(h * DH, DH), DH)
 
     def states(into, first):
-        @pl.loop(0, 8)
+        @pl.loop(0, 8, unroll=4)
         def _(i):
             h = first + i
             values = v[:, cols(h)]
@@ -171,7 +171,8 @@
         index = list(at) + [c]
         index[order[0]] = coord
         return remote(
-            wbuf.at[:, low : low + wide], w_all.at[tuple(index) + (slice(None), slice(low, low + wide))],
+            w_all.at[x, y, z, c, :, low : low + wide],
+            w_all.at[tuple(index) + (slice(None), slice(low, low + wide))],
             w_send.at[colour, 0, step], w_recv.at[colour, 0, step], {names[order[0]]: near(order[0], step)},
         )
 
@@ -218,7 +219,7 @@
         started.append(copy)
         twins.append((where[:3] + (1 - c,) + where[4:], slot))
 
-    def ring_end(group):
+    def ring_near(group):
         for colour in range(3):
             axis = COLOURS[colour][2][phase_of(group)]
             for slot in (1, 3):
@@ -226,6 +227,8 @@
                 ring_copy(colour, group, slot, step, near(axis, 4 - step), half).wait_recv()
             twin(piece(colour, group, near(axis, 1), None), 18 * colour + 3 * group)
             twin(piece(colour, group, near(axis, 3), None), 18 * colour + 3 * group + 1)
+
+    def ring_far(group):
         for colour in range(3):
             axis = COLOURS[colour][2][phase_of(group)]
             for slot in (4, 5):
@@ -241,13 +244,13 @@
     pl.semaphore_wait(barrier, 10)
     loads[0].wait()
     line_start()
-    own_store = pltpu.make_async_copy(wbuf, w_all.at[x, y, z, c], store_sem.at[2])
-    own_store.start()
     loads[1].wait()
     loads[2].wait()
     states(s_out, (1 - c) * 8)
     core_copy = remote(s_out, s_in, c_send, c_recv, {C: 1 - c})
     core_copy.start()
+    line_end()
+    ring_start(1)
     states(s_own, c * 8)
     core_copy.wait()
 
@@ -277,13 +280,12 @@
     ])
     loads[3].wait()
     loads[4].wait()
-    own_store.wait()
-    line_end()
-    ring_start(1)
-    attend(0, 2)
     ring_pass(1)
-    ring_start(2)
-    attend(2, 5)
+    ring_near(1)
+    ring_start(3)
+    attend(0, 3)
+    ring_start(5)
+    attend(3, 5)
     settle(line_copies)
 
     two = [rates[c * 8 + z * 2 + j] for j in range(2)]
@@ -330,9 +332,9 @@
                 term = held(step, j) * decay(two[j], jnp.where(spot < target, n, FAR))
                 total = term if total is None else total + term
             p_part[t, halves[j], :] = total
-    ring_end(1)
-    ring_start(3)
-    ring_pass(2)
+    ring_pass(3)
+    ring_far(1)
+    ring_start(4)
     attend(5, 8)
     settle(column_copies)
 
@@ -396,10 +398,11 @@
             )
         ]
     )
-    ring_end(2)
-    ring_start(5)
-    ring_pass(3)
-    attend(8, 11)
+    ring_pass(5)
+    ring_start(2)
+    attend(8, 9)
+    ring_pass(4)
+    attend(9, 11)
     settle(slab_copies)
 
     total = jnp.zeros((DH, DH), F32)
@@ -428,10 +431,16 @@
         )
         for step in (1, 3, 2)
     ])
-    ring_end(3)
-    ring_start(4)
-    ring_pass(5)
-    attend(11, 16)
+    ring_near(3)
+    ring_far(3)
+    ring_near(5)
+    ring_far(5)
+    attend(11, 12)
+    ring_pass(2)
+    attend(12, 14)
+    ring_near(4)
+    ring_far(4)
+    attend(14, 16)
     settle(back_copies)
 
     n_chip = same(ids[chip], ids[chip + 4], 512.0)
@@ -449,10 +458,11 @@
             c_out[i] = away.astype(BF16)
     pair_copy = remote(c_out, c_in, d_send, d_recv, {C: 1 - c})
     pair_copy.start()
-    ring_pass(4)
+    ring_near(2)
+    ring_far(2)
 
     def finish(first, ref):
-        @pl.loop(0, 8)
+        @pl.loop(0, 8, unroll=4)
         def _(i):
             h = first + i
             carried = dot(q[:, cols(h)], ref[i], 1, 0)
@@ -464,22 +474,26 @@
                 inv = lax.rsqrt(jnp.mean(mixed * mixed, axis=-1, keepdims=True) + 1e-06)
                 nrm[part, cols(h)] = (mixed * inv * gated[h, part, :]).astype(BF16)
 
-    def put(first, slot):
-        half = pl.ds(pl.multiple_of(first * DH, 1024), 1024)
-        return pltpu.make_async_copy(nrm.at[:, half], nrm_hbm.at[:, half], store_sem.at[slot])
-
     finish(c * 8, p_own)
-    put(c * 8, 0).start()
-    ring_end(5)
-    ring_end(4)
     pair_copy.wait()
     finish((1 - c) * 8, c_in)
-    put((1 - c) * 8, 1).start()
     twin_waits()
+
+    def leave(n):
+        lanes = pl.ds(pl.multiple_of(n * 512, 512), 512)
+        return pltpu.make_async_copy(mixed_out.at[:, lanes], out_hbm.at[:, lanes], store_sem.at[n])
+
+    @pl.loop(0, 4)
+    def _(n):
+        lanes = pl.ds(pl.multiple_of(n * 512, 512), 512)
+        weight = w_all[:, :, :, :, :, lanes].reshape(2048, 512)
+        mixed_out[:, lanes] = dot(nrm[...], weight, 1, 0).astype(BF16)
+        leave(n).start()
+
     for copy in started:
         copy.wait_send()
-    put(c * 8, 0).wait()
-    put((1 - c) * 8, 1).wait()
+    for n in range(4):
+        leave(n).wait()
 
 
 def gather_and_attend(ids, rates, q, k, v, g, gain, w):
@@ -492,18 +506,16 @@
     rows = w.shape[0]
     return pl.pallas_call(
         scan_kernel,
-        out_shape=(
-            jax.ShapeDtypeStruct((tokens, width), BF16),
-            jax.ShapeDtypeStruct((4, 4, 4, 2, rows, width), BF16),
-        ),
+        out_shape=jax.ShapeDtypeStruct((tokens, width), BF16),
         in_specs=[smem, smem, hbm, hbm, hbm, hbm, pl.BlockSpec(memory_space=vmem), hbm],
-        out_specs=(hbm, hbm),
+        out_specs=hbm,
         scratch_shapes=[
             vmem((tokens, width), BF16),
             vmem((tokens, width), BF16),
             vmem((tokens, width), BF16),
             vmem((tokens, width), BF16),
-            vmem((rows, width), BF16),
+            vmem((4, 4, 4, 2, rows, width), BF16),
+            vmem((tokens, width), BF16),
             vmem((tokens, width), BF16),
             vmem((heads, tokens, DH), F32),
             vmem((heads, tokens, DH), F32),
@@ -529,7 +541,7 @@
             vmem((8, DH, DH), BF16),
             vmem((8, DH, DH), BF16),
             dma((5,)),
-            dma((3,)),
+            dma((8,)),
             dma, dma,
             dma((3,)), dma((3,)),
             dma((3,)), dma((3,)),
@@ -548,35 +560,12 @@
     )(ids, rates, q, k, v, g, gain, w)
 
 
-def project_kernel(a, b, o):
-    o[...] = jnp.dot(a[...], b[...], preferred_element_type=F32).astype(BF16)
-
-
-def project(a, b):
-    rows, depth = a.shape
-    columns = b.shape[1]
-    tile = 1024
-    return pl.pallas_call(
-        project_kernel,
-        out_shape=jax.ShapeDtypeStruct((rows, columns), BF16),
-        grid=(columns // tile,),
-        in_specs=[
-            pl.BlockSpec((rows, depth), lambda j: (0, 0)),
-            pl.BlockSpec((depth, tile), lambda j: (0, j)),
-        ],
-        out_specs=pl.BlockSpec((rows, tile), lambda j: (0, j)),
-        compiler_params=pltpu.CompilerParams(vmem_limit_bytes=60 << 20),
-        name="project",
-    )(a, b)
-
-
 def on_device(query_rows, key_rows, value_rows, gate_rows, segment_ids, decay_rates, norm_gain, out_weight):
     width = query_rows.shape[1]
-    normed, weight = gather_and_attend(
+    return gather_and_attend(
         segment_ids, decay_rates, query_rows, key_rows, value_rows, gate_rows,
         norm_gain.reshape(1, width), out_weight,
     )
-    return project(normed, weight.reshape(width, width))
 
 
 def solution(mesh):

time: 57.7 us -> 52.1 us (0.903)
  Pallas kernels: 57.5 us -> 48.7 us
  local copies, waits for them, and re-layouts: 0 us -> 3.16 us
    pallas_call x2 -> x1, Pallas kernels: 57.5 us -> 48.7 us  [gather_and_attend(): pl.pallas_call(scan_kernel, out_shape=jax.ShapeDtypeStruct((tokens, width...]
    unnamed x0 -> x1, local copies, waits for them, and re-layouts: none -> 3.16 us
where the time goes in v4:
time: 52.1 us; the launch traced here: 51.9 us
  Pallas kernels  48.7 us (93%)
  local copies, waits for them, and re-layouts  3.16 us (6%)
    pallas_call x1, Pallas kernels, gather_and_attend(): pl.pallas_call(scan_kernel, out_shape=jax.ShapeDtypeStruct((tokens, width...  48.7 us
    unnamed x1, local copies, waits for them, and re-layouts  3.16 us

profile of v4, /device:TPU:1, one launch (start us, length us, event | category | flops | bytes accessed | tf_op | source)
XLA Modules:
  0.0 51.9 jit_solution(13547995833552530077)
XLA Ops:
  0.0 48.7 %scan_and_gather.1 = bf16[512,2048]{1,0:T(8,128)(2,1)} custom-call(s32[32]{0:T(128)} %ids.1, f32[16]{0:T(128)} %rates.1, bf16[512,2048]{1,0:T(8,128)(2,1)} %q_hbm.1, bf16[512,2048]{1,0:T(8,128)(2,1)} %k_hbm.1, bf16[512,2048]{1,0:T(8,128)(2,1)} %v_hbm.1, bf16[512,2048]{1,0:T(8,128)(2,1)} %g_hbm.1, f32[1,2048]{1,0:T(1,128)} %bitcast.1, bf16[16,2048]{1,0:T(8,128)(2,1)} %w_in.1), custom_call_target="tpu_custom_call" | custom-call | tf_op jit(solution)/shard_map/scan_and_gather/pallas_call | solution.py:507
  48.7 3.2 %copy.10 = bf16[512,2048]{1,0:T(8,128)(2,1)} copy(bf16[512,2048]{1,0:T(8,128)(2,1)} %scan_and_gather.1) | data formatting | bytes 4194304

commit v5 on v4

--- a/solution.py
+++ b/solution.py
@@ -38,12 +38,12 @@
 
 
 def scan_kernel(
-    ids, rates, q_hbm, k_hbm, v_hbm, g_hbm, gain, w_in,
-    out_hbm,
-    q, k, v, g, w_all, nrm, mixed_out, inner, gated, keep_n, lasting,
+    ids_hbm, rates_hbm, q_hbm, k_hbm, v_hbm, g_hbm, gain_hbm, w_in,
+    mixed_out,
+    ids, rates, gain, q, k, v, g, w_all, nrm, inner, gated, keep_n, lasting,
     s_own, s_out, s_in, z_out, z_in, p_part, y_out, y_in, x_out, x_in, u_out, u_in, m_out, m_in,
     p_out, p_in, c_out, c_in, p_own,
-    load_sem, store_sem, c_send, c_recv, z_send, z_recv, y_send, y_recv, x_send, x_recv,
+    load_sem, c_send, c_recv, z_send, z_recv, y_send, y_recv, x_send, x_recv,
     u_send, u_recv, m_send, m_recv, p_send, p_recv, d_send, d_recv, w_send, w_recv, b_send, b_recv,
 ):
     at = (lax.axis_index(X), lax.axis_index(Y), lax.axis_index(Z))
@@ -64,11 +64,14 @@
     loads = [
         pltpu.make_async_copy(src, dst, load_sem.at[n])
         for n, (src, dst) in enumerate(
-            ((w_in, w_all.at[x, y, z, c]), (k_hbm, k), (v_hbm, v), (q_hbm, q), (g_hbm, g))
+            ((w_in, w_all.at[x, y, z, c]), (k_hbm, k), (v_hbm, v), (q_hbm, q), (g_hbm, g),
+             (ids_hbm, ids), (rates_hbm, rates), (gain_hbm, gain))
         )
     ]
-    for load in loads:
-        load.start()
+    for n in (5, 6, 0, 1, 2, 3, 4, 7):
+        loads[n].start()
+    loads[5].wait()
+    loads[6].wait()
 
     place = z * 2 + c
     own_id = [ids[place * 4 + b] for b in range(4)]
@@ -280,6 +283,7 @@
     ])
     loads[3].wait()
     loads[4].wait()
+    loads[7].wait()
     ring_pass(1)
     ring_near(1)
     ring_start(3)
@@ -479,27 +483,20 @@
     finish((1 - c) * 8, c_in)
     twin_waits()
 
-    def leave(n):
-        lanes = pl.ds(pl.multiple_of(n * 512, 512), 512)
-        return pltpu.make_async_copy(mixed_out.at[:, lanes], out_hbm.at[:, lanes], store_sem.at[n])
-
     @pl.loop(0, 4)
     def _(n):
         lanes = pl.ds(pl.multiple_of(n * 512, 512), 512)
         weight = w_all[:, :, :, :, :, lanes].reshape(2048, 512)
         mixed_out[:, lanes] = dot(nrm[...], weight, 1, 0).astype(BF16)
-        leave(n).start()
 
     for copy in started:
         copy.wait_send()
-    for n in range(4):
-        leave(n).wait()
 
 
 def gather_and_attend(ids, rates, q, k, v, g, gain, w):
     tokens, width = q.shape
     heads = rates.shape[0]
-    hbm = pl.BlockSpec(memory_space=pl.ANY)
+    hbm = pl.BlockSpec(memory_space=pltpu.HBM)
     smem = pl.BlockSpec(memory_space=pltpu.SMEM)
     vmem = pltpu.VMEM
     dma = pltpu.SemaphoreType.DMA
@@ -507,15 +504,17 @@
     return pl.pallas_call(
         scan_kernel,
         out_shape=jax.ShapeDtypeStruct((tokens, width), BF16),
-        in_specs=[smem, smem, hbm, hbm, hbm, hbm, pl.BlockSpec(memory_space=vmem), hbm],
-        out_specs=hbm,
+        in_specs=[hbm] * 8,
+        out_specs=pl.BlockSpec(memory_space=vmem),
         scratch_shapes=[
+            pltpu.SMEM((32,), jnp.int32),
+            pltpu.SMEM((16,), F32),
+            vmem((1, width), F32),
             vmem((tokens, width), BF16),
             vmem((tokens, width), BF16),
             vmem((tokens, width), BF16),
             vmem((tokens, width), BF16),
             vmem((4, 4, 4, 2, rows, width), BF16),
-            vmem((tokens, width), BF16),
             vmem((tokens, width), BF16),
             vmem((heads, tokens, DH), F32),
             vmem((heads, tokens, DH), F32),
@@ -540,7 +539,6 @@
             vmem((8, DH, DH), BF16),
             vmem((8, DH, DH), BF16),
             vmem((8, DH, DH), BF16),
-            dma((5,)),
             dma((8,)),
             dma, dma,
             dma((3,)), dma((3,)),
@@ -554,10 +552,10 @@
             dma((54,)), dma((54,)),
         ],
         compiler_params=pltpu.CompilerParams(
-            collective_id=0, has_side_effects=True, vmem_limit_bytes=60 << 20
+            collective_id=0, has_side_effects=True, vmem_limit_bytes=48 << 20
         ),
         name="scan_and_gather",
-    )(ids, rates, q, k, v, g, gain, w)
+    )(*(pltpu.with_memory_space_constraint(a, pltpu.HBM) for a in (ids, rates, q, k, v, g, gain, w)))
 
 
 def on_device(query_rows, key_rows, value_rows, gate_rows, segment_ids, decay_rates, norm_gain, out_weight):

time: 52.1 us -> 48.8 us (0.937)
  local copies, waits for them, and re-layouts: 3.16 us -> 1.32 us
  Pallas kernels: 48.7 us -> 47.3 us
    unnamed x1, local copies, waits for them, and re-layouts: 3.16 us -> 1.32 us
    pallas_call x1, Pallas kernels: 48.7 us -> 47.3 us  [gather_and_attend(): pl.pallas_call(scan_kernel, out_shape=jax.ShapeDtypeStruct((tokens, width...]
where the time goes in v5:
time: 48.8 us; the launch traced here: 48.7 us
  Pallas kernels  47.3 us (97%)
  local copies, waits for them, and re-layouts  1.32 us (3%)
    pallas_call x1, Pallas kernels, gather_and_attend(): pl.pallas_call(scan_kernel, out_shape=jax.ShapeDtypeStruct((tokens, width...  47.3 us
    unnamed x1, local copies, waits for them, and re-layouts  1.32 us

profile of v5, /device:TPU:1, one launch (start us, length us, event | category | flops | bytes accessed | tf_op | source)
XLA Modules:
  0.0 48.7 jit_solution(7600480501572567961)
XLA Ops:
  0.0 47.3 %scan_and_gather.1 = bf16[512,2048]{1,0:T(8,128)(2,1)S(1)} custom-call(s32[32]{0:T(128)} %ids_hbm.1, f32[16]{0:T(128)} %rates_hbm.1, bf16[512,2048]{1,0:T(8,128)(2,1)} %q_hbm.1, bf16[512,2048]{1,0:T(8,128)(2,1)} %k_hbm.1, bf16[512,2048]{1,0:T(8,128)(2,1)} %v_hbm.1, bf16[512,2048]{1,0:T(8,128)(2,1)} %g_hbm.1, f32[1,2048]{1,0:T(1,128)} %bitcast.1, ...), custom_call_target="tpu_custom_call" | custom-call | tf_op jit(solution)/shard_map/scan_and_gather/pallas_call | solution.py:504
  47.3 1.3 %copy.10 = bf16[512,2048]{1,0:T(8,128)(2,1)} copy(bf16[512,2048]{1,0:T(8,128)(2,1)S(1)} %scan_and_gather.1) | data formatting | bytes 4194304

commit v6 on v5

--- a/solution.py
+++ b/solution.py
@@ -483,7 +483,7 @@
     finish((1 - c) * 8, c_in)
     twin_waits()
 
-    @pl.loop(0, 4)
+    @pl.loop(0, 4, unroll=2)
     def _(n):
         lanes = pl.ds(pl.multiple_of(n * 512, 512), 512)
         weight = w_all[:, :, :, :, :, lanes].reshape(2048, 512)

time: 48.8 us -> 48.4 us (level)
  no operation moved by 1% of the time
where the time goes in v6:
time: 48.4 us; the launch traced here: 48.3 us
  Pallas kernels  47 us (97%)
  local copies, waits for them, and re-layouts  1.32 us (3%)
    pallas_call x1, Pallas kernels, gather_and_attend(): pl.pallas_call(scan_kernel, out_shape=jax.ShapeDtypeStruct((tokens, width...  47 us
    unnamed x1, local copies, waits for them, and re-layouts  1.32 us

profile of v6, /device:TPU:1, one launch (start us, length us, event | category | flops | bytes accessed | tf_op | source)
XLA Modules:
  0.0 48.3 jit_solution(1290144310446582154)
XLA Ops:
  0.0 47.0 %scan_and_gather.1 = bf16[512,2048]{1,0:T(8,128)(2,1)S(1)} custom-call(s32[32]{0:T(128)} %ids_hbm.1, f32[16]{0:T(128)} %rates_hbm.1, bf16[512,2048]{1,0:T(8,128)(2,1)} %q_hbm.1, bf16[512,2048]{1,0:T(8,128)(2,1)} %k_hbm.1, bf16[512,2048]{1,0:T(8,128)(2,1)} %v_hbm.1, bf16[512,2048]{1,0:T(8,128)(2,1)} %g_hbm.1, f32[1,2048]{1,0:T(1,128)} %bitcast.1, ...), custom_call_target="tpu_custom_call" | custom-call | tf_op jit(solution)/shard_map/scan_and_gather/pallas_call | solution.py:504
  47.0 1.3 %copy.10 = bf16[512,2048]{1,0:T(8,128)(2,1)} copy(bf16[512,2048]{1,0:T(8,128)(2,1)S(1)} %scan_and_gather.1) | data formatting | bytes 4194304
